TPU v7x, 32 devices: a whole 2x2x4 slice. The times are simulated.
32 devices in a mesh: gx: 8 (over z, y), gy: 4 (over x, core).
Axes of the slice: x: 2, y: 2, z: 4, core: 2. Of those that a mesh axis runs over, the one named last changes fastest.
Arguments:
- magnet: float32 [3, 32, 2048], P(None, 'gx', 'gy'), may hold values from -1 to 1, as said below
- thermal: float32 [3, 3, 32, 2048], P(None, None, 'gx', 'gy'), may hold values from -4 to 4
- kernel_diag: float32 [3, 128, 64, 64], P(None, 'gy', 'gx'), may hold values from 0.05 to 0.6, as said below
- kernel_off: float32 [3, 128, 64, 64], P(None, 'gy', 'gx'), may hold values from -0.25 to 0.25, as said below
Outputs:
- final_magnet: float32 [3, 32, 2048], P(None, 'gx', 'gy')
- demag_field: float32 [3, 32, 2048], P(None, 'gx', 'gy')
Inputs may be any that keep to these rules, and one draw needn't show every extreme that they name: `magnet`: each cell's three components form a unit vector. `kernel_diag`: each entry at (kz, ky, kx) equals the entry at (-kz, -ky, -kx), indices taken modulo 2 * 64, 64, 64. `kernel_off`: each entry at (kz, ky, kx) equals the entry at (-kz, -ky, -kx), indices taken modulo 2 * 64, 64, 64.
All inputs are finite; a program needn't handle non-finite values.
Results may differ from a plain program's by a relative error of at most 0.0001.
Values sent between devices are 32-bit elements; how exact they have to be, the bound alone decides.
A program may use at most 64 MiB of HBM per device.

v0:
```python
import math

import jax
import jax.numpy as jnp
from jax import lax
from jax.sharding import PartitionSpec as P

NZ = 64
STEPS = 3


damping = 0.1
time_step = 0.05
anisotropy = 0.5


def with_halo(x, sides, width):
    for axis, dim in sides:
        count, length = (lax.axis_size(axis), x.shape[dim])
        up = [(i, (i + 1) % count) for i in range(count - 1)]
        down = [(j, i) for i, j in up]
        last = lax.slice_in_dim(x, length - width, length, axis=dim)
        first = lax.slice_in_dim(x, 0, width, axis=dim)
        before = lax.ppermute(last, axis, up)
        after = lax.ppermute(first, axis, down)
        x = jnp.concatenate([before, x, after], axis=dim)
    return x


def twiddle(first_idx, second_idx, period):
    phase = first_idx[:, None] * second_idx[None, :] % period
    angle = phase.astype(jnp.float32) * (2.0 * math.pi / period)
    return (jnp.cos(angle), jnp.sin(angle))


def counting(length):
    return jnp.arange(length, dtype=jnp.int32)


def contract(form, data, table):
    return jnp.einsum(
        form, data, table, precision=lax.Precision.HIGHEST, preferred_element_type=jnp.float32
    )


def cross(left, right):
    return jnp.stack(
        [
            left[1] * right[2] - left[2] * right[1],
            left[2] * right[0] - left[0] * right[2],
            left[0] * right[1] - left[1] * right[0],
        ]
    )


def torque(field, heff):
    first = cross(field, heff)
    return -(first + damping * cross(field, first)) / (1.0 + damping * damping)


def edge_fix(extended, width):
    x_index = lax.axis_index("gx")
    y_index = lax.axis_index("gy")
    x_last = lax.axis_size("gx") - 1
    y_last = lax.axis_size("gy") - 1
    low = jnp.where(
        x_index == 0, jnp.repeat(extended[:, width : width + 1], width, axis=1), extended[:, :width]
    )
    high = jnp.where(
        x_index == x_last,
        jnp.repeat(extended[:, -width - 1 : -width], width, axis=1),
        extended[:, -width:],
    )
    extended = jnp.concatenate([low, extended[:, width:-width], high], axis=1)
    low = jnp.where(
        y_index == 0,
        jnp.repeat(extended[:, :, width : width + 1], width, axis=2),
        extended[:, :, :width],
    )
    high = jnp.where(
        y_index == y_last,
        jnp.repeat(extended[:, :, -width - 1 : -width], width, axis=2),
        extended[:, :, -width:],
    )
    return jnp.concatenate([low, extended[:, :, width:-width], high], axis=2)


def laplace(extended):
    center = extended[:, 1:-1, 1:-1]
    z_plus = jnp.concatenate([center[..., 1:], center[..., -1:]], axis=3)
    z_minus = jnp.concatenate([center[..., :1], center[..., :-1]], axis=3)
    total = extended[:, 2:, 1:-1] + extended[:, :-2, 1:-1]
    total = total + extended[:, 1:-1, 2:] + extended[:, 1:-1, :-2]
    total = total + z_plus + z_minus
    return total - 6.0 * center


def effective(field, laplacian, demag, noise):
    heff = laplacian + demag + noise
    return heff.at[2].add(anisotropy * field[2])


def demagnetize(field, kernel_diag, kernel_off):
    depth = field.shape[3]
    y_devices = lax.axis_size("gy")
    block = 2 * depth // y_devices
    offsets = counting(block)
    weights = jnp.ones((block,), jnp.float32)
    kept = (block * counting(y_devices)[:, None] + offsets[None, :]).reshape(-1)
    kept_weights = jnp.tile(weights, y_devices)
    z_cos, z_sin = twiddle(counting(depth), kept, 2 * depth)
    z_real = contract("cxyz,zk->cxky", field, z_cos)
    z_imag = -contract("cxyz,zk->cxky", field, z_sin)
    y_pencil = lax.all_to_all(
        jnp.stack([z_real, z_imag]), "gy", split_axis=3, concat_axis=4, tiled=True
    )
    full_y = y_pencil.shape[4]
    y_cos, y_sin = twiddle(counting(full_y), counting(2 * full_y), 2 * full_y)
    real_part, imag_part = (y_pencil[0], y_pencil[1])
    y_real = contract("cxqy,yk->cqkx", real_part, y_cos) + contract(
        "cxqy,yk->cqkx", imag_part, y_sin
    )
    y_imag = contract("cxqy,yk->cqkx", imag_part, y_cos) - contract(
        "cxqy,yk->cqkx", real_part, y_sin
    )
    x_pencil = lax.all_to_all(
        jnp.stack([y_real, y_imag]), "gx", split_axis=3, concat_axis=4, tiled=True
    )
    full_x = x_pencil.shape[4]
    x_cos, x_sin = twiddle(counting(full_x), counting(2 * full_x), 2 * full_x)
    real_part, imag_part = (x_pencil[0], x_pencil[1])
    x_real = contract("cqkx,xj->cqkj", real_part, x_cos) + contract(
        "cqkx,xj->cqkj", imag_part, x_sin
    )
    x_imag = contract("cqkx,xj->cqkj", imag_part, x_cos) - contract(
        "cqkx,xj->cqkj", real_part, x_sin
    )

    def apply_tensor(spectra):
        first = (
            kernel_diag[0] * spectra[0] + kernel_off[0] * spectra[1] + kernel_off[1] * spectra[2]
        )
        second = (
            kernel_off[0] * spectra[0] + kernel_diag[1] * spectra[1] + kernel_off[2] * spectra[2]
        )
        third = (
            kernel_off[1] * spectra[0] + kernel_off[2] * spectra[1] + kernel_diag[2] * spectra[2]
        )
        return -jnp.stack([first, second, third])

    h_real = apply_tensor(x_real)
    h_imag = apply_tensor(x_imag)
    back_cos, back_sin = twiddle(counting(2 * full_x), counting(full_x), 2 * full_x)
    back_real = contract("cqkj,jx->cqkx", h_real, back_cos) - contract(
        "cqkj,jx->cqkx", h_imag, back_sin
    )
    back_imag = contract("cqkj,jx->cqkx", h_imag, back_cos) + contract(
        "cqkj,jx->cqkx", h_real, back_sin
    )
    y_rows = lax.all_to_all(
        jnp.stack([back_real, back_imag]), "gx", split_axis=4, concat_axis=3, tiled=True
    )
    real_part, imag_part = (y_rows[0], y_rows[1])
    scale = 1.0 / (8.0 * full_x * full_y * depth)
    inv_cos, inv_sin = twiddle(counting(2 * full_y), counting(full_y), 2 * full_y)
    g_real = contract("cqkx,kv->cxvq", real_part, inv_cos) - contract(
        "cqkx,kv->cxvq", imag_part, inv_sin
    )
    g_imag = contract("cqkx,kv->cxvq", imag_part, inv_cos) + contract(
        "cqkx,kv->cxvq", real_part, inv_sin
    )
    z_rows = lax.all_to_all(
        jnp.stack([g_real, g_imag]), "gy", split_axis=3, concat_axis=4, tiled=True
    )
    last_cos, last_sin = twiddle(kept, counting(depth), 2 * depth)
    last_cos = last_cos * kept_weights[:, None]
    last_sin = last_sin * kept_weights[:, None]
    demag = contract("cxyk,kz->cxyz", z_rows[0], last_cos) - contract(
        "cxyk,kz->cxyz", z_rows[1], last_sin
    )
    return demag * scale


def body(magnet, thermal, kernel_diag, kernel_off):
    comps, local_x, flat = magnet.shape
    local_y = flat // NZ
    field = magnet.reshape(3, local_x, local_y, NZ)
    demag = demagnetize(field, kernel_diag, kernel_off)
    demag_wide = with_halo(demag, (("gx", 1), ("gy", 2)), 1)
    for step in range(STEPS):
        noise = thermal[step].reshape(3, local_x, local_y, NZ)
        stacked = with_halo(jnp.concatenate([field, noise]), (("gx", 1), ("gy", 2)), 2)
        stacked = edge_fix(stacked, 2)
        field_wide = stacked[:3, 1:-1, 1:-1]
        noise_wide = stacked[3:, 1:-1, 1:-1]
        first_wide = torque(
            field_wide, effective(field_wide, laplace(stacked[:3]), demag_wide, noise_wide)
        )
        trial_wide = edge_fix(field_wide + time_step * first_wide, 1)
        trial = trial_wide[:, 1:-1, 1:-1]
        second = torque(trial, effective(trial, laplace(trial_wide), demag, noise))
        first = first_wide[:, 1:-1, 1:-1]
        update = field + 0.5 * time_step * (first + second)
        field = update / jnp.sqrt(jnp.sum(update * update, axis=0, keepdims=True))
    return (field.reshape(3, local_x, flat), demag.reshape(3, local_x, flat))


def solution(mesh):
    in_specs = (
        P(None, "gx", "gy"),
        P(None, None, "gx", "gy"),
        P(None, "gy", "gx", None),
        P(None, "gy", "gx", None),
    )
    out_specs = (P(None, "gx", "gy"), P(None, "gx", "gy"))
    return jax.shard_map(body, mesh=mesh, in_specs=in_specs, out_specs=out_specs, check_vma=False)
```

profile of v0, /device:TPU:1, one launch (start us, length us, event | category | flops | bytes accessed | tf_op | source)
XLA Modules:
  0.0 136.8 jit_solution(13269191721414528396)
XLA Ops:
  0.6 0.8 reshape.316
  1.5 1.4 %fusion.276 = (f32[1,3,4,512]{3,2,1,0:T(4,128)}, f32[1,3,4,512]{3,2,1,0:T(4,128)S(1)}, f32[1,3,4,512]{3,2,1,0:T(4,128)S(1)}) fusion(f32[3,3,4,512]{3,2,1,0:T(4,128)} %param.17), kind=kLoop, calls=%fused_computation.453 | loop fusion | bytes 147456 | tf_op jit(solution)/shard_map/slice | solution.py:191
  3.0 4.0 %collective-permute-start = (f32[6,2,8,64]{3,2,1,0:T(8,128)S(1)}, f32[6,2,8,64]{3,2,1,0:T(8,128)S(1)}, u32[]{:S(2)}, u32[]{:S(2)}) collective-permute-start(f32[6,2,8,64]{3,2,1,0:T(8,128)S(1)} %get-tuple-element.200), channel_id=1, source_target_pairs={{0,4},{4,8},{8,12},{12,16},{16,20},{20,24},{24,28},{1,5},{5,9},{9,... | collective-permute-start | bytes 73736 | tf_op jit(solution)/shard_map/ppermute | solution.py:24
  7.0 1.3 collective-permute-start.1
  9.3 0.7 copy.77
  10.1 2.4 %reshape.351 = f32[4,1,6144]{2,1,0:T(1,128)} reshape(f32[128,2,3,4,8]{4,3,2,1,0:T(4,128)S(1)} %bitcast.168) | data formatting | bytes 196608
  12.5 4.2 %all-to-all-start = ((f32[4,1,6144]{2,1,0:T(1,128)}), f32[4,1,6144]{2,1,0:T(1,128)S(1)}, u32[]{:S(2)}, u32[]{:S(2)}) async-start(f32[4,1,6144]{2,1,0:T(1,128)} %reshape.351), calls=%async_computation | async-start | bytes 196608 | tf_op jit(solution)/shard_map/all_to_all | solution.py:114
  16.8 3.5 %collective-permute-start.2 = (f32[6,8,2,64]{3,2,1,0:T(2,128)S(1)}, f32[6,8,2,64]{3,2,1,0:T(2,128)S(1)}, u32[]{:S(2)}, u32[]{:S(2)}) collective-permute-start(f32[6,8,2,64]{3,2,1,0:T(2,128)S(1)} %get-tuple-element.170), channel_id=1, source_target_pairs={{0,1},{1,2},{2,3},{4,5},{5,6},{6,7},{8,9},{9,10},{10,11},{12,13},{... | collective-permute-start | bytes 73736 | tf_op jit(solution)/shard_map/ppermute | solution.py:24
  20.3 1.9 %collective-permute-start.3 = (f32[6,8,2,64]{3,2,1,0:T(2,128)S(1)}, f32[6,8,2,64]{3,2,1,0:T(2,128)S(1)}, u32[]{:S(2)}, u32[]{:S(2)}) collective-permute-start(f32[6,8,2,64]{3,2,1,0:T(2,128)S(1)} %get-tuple-element.171), channel_id=1, source_target_pairs={{1,0},{2,1},{3,2},{5,4},{6,5},{7,6},{9,8},{10,9},{11,10},{13,12},{... | collective-permute-start | bytes 73736 | tf_op jit(solution)/shard_map/ppermute | solution.py:25
  22.3 0.7 fusion.264
  23.1 2.7 %collective-permute-done.3 = f32[6,8,2,64]{3,2,1,0:T(2,128)S(1)} collective-permute-done((f32[6,8,2,64]{3,2,1,0:T(2,128)S(1)}, f32[6,8,2,64]{3,2,1,0:T(2,128)S(1)}, u32[]{:S(2)}, u32[]{:S(2)}) %collective-permute-start.3) | collective-permute-done | bytes 24608 | tf_op jit(solution)/shard_map/ppermute | solution.py:25
  25.8 0.6 copy-done.11
  27.0 0.9 reduce.12
  27.9 1.9 %reshape.352 = f32[128,2,3,4,8]{4,3,2,1,0:T(4,128)S(1)} reshape(f32[4,6144]{1,0:T(4,128)S(1)} %reduce.12) | data formatting | bytes 196608
  29.8 0.7 copy.124
  33.0 1.2 reshape.353
  34.2 6.7 %all-to-all-start.1 = ((f32[8,1,6144]{2,1,0:T(1,128)}), f32[8,1,6144]{2,1,0:T(1,128)S(1)}, u32[]{:S(2)}, u32[]{:S(2)}) async-start(f32[8,1,6144]{2,1,0:T(1,128)} %reshape.353), calls=%async_computation.1 | async-start | bytes 393216 | tf_op jit(solution)/shard_map/all_to_all | solution.py:126
  41.0 6.6 %all-to-all-done.1 = f32[8,1,6144]{2,1,0:T(1,128)S(1)} async-done(((f32[8,1,6144]{2,1,0:T(1,128)}), f32[8,1,6144]{2,1,0:T(1,128)S(1)}, u32[]{:S(2)}, u32[]{:S(2)}) %all-to-all-start.1) | async-done | bytes 196640 | tf_op jit(solution)/shard_map/all_to_all | solution.py:126
  47.6 1.1 reduce.13
  54.0 0.5 fusion
  55.0 1.0 reshape.355
  56.0 3.4 %all-to-all-start.2 = ((f32[8,1,6144]{2,1,0:T(1,128)}), f32[8,1,6144]{2,1,0:T(1,128)S(1)}, u32[]{:S(2)}, u32[]{:S(2)}) async-start(f32[8,1,6144]{2,1,0:T(1,128)} %reshape.355), calls=%async_computation.2 | async-start | bytes 393216 | tf_op jit(solution)/shard_map/all_to_all | solution.py:160
  59.7 7.4 %all-to-all-done.2 = f32[8,1,6144]{2,1,0:T(1,128)S(1)} async-done(((f32[8,1,6144]{2,1,0:T(1,128)}), f32[8,1,6144]{2,1,0:T(1,128)S(1)}, u32[]{:S(2)}, u32[]{:S(2)}) %all-to-all-start.2) | async-done | bytes 196640 | tf_op jit(solution)/shard_map/all_to_all | solution.py:160
  67.0 1.1 reduce.14
  70.5 0.9 reshape.357
  71.4 4.5 %all-to-all-start.3 = ((f32[4,1,6144]{2,1,0:T(1,128)}), f32[4,1,6144]{2,1,0:T(1,128)S(1)}, u32[]{:S(2)}, u32[]{:S(2)}) async-start(f32[4,1,6144]{2,1,0:T(1,128)} %reshape.357), calls=%async_computation.3 | async-start | bytes 196608 | tf_op jit(solution)/shard_map/all_to_all | solution.py:172
  76.1 3.3 %all-to-all-done.3 = f32[4,1,6144]{2,1,0:T(1,128)S(1)} async-done(((f32[4,1,6144]{2,1,0:T(1,128)}), f32[4,1,6144]{2,1,0:T(1,128)S(1)}, u32[]{:S(2)}, u32[]{:S(2)}) %all-to-all-start.3) | async-done | bytes 98336 | tf_op jit(solution)/shard_map/all_to_all | solution.py:172
  79.3 0.9 reduce.15
  81.7 2.6 %collective-permute-start.4 = (f32[3,1,8,64]{3,2,1,0:T(8,128)S(1)}, f32[3,1,8,64]{3,2,1,0:T(8,128)S(1)}, u32[]{:S(2)}, u32[]{:S(2)}) collective-permute-start(f32[3,1,8,64]{3,2,1,0:T(8,128)S(1)} %get-tuple-element.207), channel_id=1, source_target_pairs={{0,4},{4,8},{8,12},{12,16},{16,20},{20,24},{24,28},{1,5},{5,9},{9,... | collective-permute-start | bytes 18440 | tf_op jit(solution)/shard_map/ppermute | solution.py:24
  84.3 1.3 collective-permute-start.5
  85.7 3.0 %collective-permute-done.5 = f32[3,1,8,64]{3,2,1,0:T(8,128)S(1)} collective-permute-done((f32[3,1,8,64]{3,2,1,0:T(8,128)S(1)}, f32[3,1,8,64]{3,2,1,0:T(8,128)S(1)}, u32[]{:S(2)}, u32[]{:S(2)}) %collective-permute-start.5) | collective-permute-done | bytes 6176 | tf_op jit(solution)/shard_map/ppermute | solution.py:25
  88.8 4.5 %collective-permute-start.6 = (f32[3,6,1,64]{3,2,1,0:T(1,128)S(1)}, f32[3,6,1,64]{3,2,1,0:T(1,128)S(1)}, u32[]{:S(2)}, u32[]{:S(2)}) collective-permute-start(f32[3,6,1,64]{3,2,1,0:T(1,128)S(1)} %get-tuple-element.205), channel_id=1, source_target_pairs={{0,1},{1,2},{2,3},{4,5},{5,6},{6,7},{8,9},{9,10},{10,11},{12,13},{... | collective-permute-start | bytes 13832 | tf_op jit(solution)/shard_map/ppermute | solution.py:24
  93.2 1.9 %collective-permute-start.7 = (f32[3,6,1,64]{3,2,1,0:T(1,128)S(1)}, f32[3,6,1,64]{3,2,1,0:T(1,128)S(1)}, u32[]{:S(2)}, u32[]{:S(2)}) collective-permute-start(f32[3,6,1,64]{3,2,1,0:T(1,128)S(1)} %get-tuple-element.206), channel_id=1, source_target_pairs={{1,0},{2,1},{3,2},{5,4},{6,5},{7,6},{9,8},{10,9},{11,10},{13,12},{... | collective-permute-start | bytes 13832 | tf_op jit(solution)/shard_map/ppermute | solution.py:25
  95.3 2.9 %collective-permute-done.7 = f32[3,6,1,64]{3,2,1,0:T(1,128)S(1)} collective-permute-done((f32[3,6,1,64]{3,2,1,0:T(1,128)S(1)}, f32[3,6,1,64]{3,2,1,0:T(1,128)S(1)}, u32[]{:S(2)}, u32[]{:S(2)}) %collective-permute-start.7) | collective-permute-done | bytes 4640 | tf_op jit(solution)/shard_map/ppermute | solution.py:25
  99.5 2.9 %collective-permute-start.8 = (f32[6,2,8,64]{3,2,1,0:T(8,128)S(1)}, f32[6,2,8,64]{3,2,1,0:T(8,128)S(1)}, u32[]{:S(2)}, u32[]{:S(2)}) collective-permute-start(f32[6,2,8,64]{3,2,1,0:T(8,128)S(1)} %get-tuple-element.198), channel_id=1, source_target_pairs={{0,4},{4,8},{8,12},{12,16},{16,20},{20,24},{24,28},{1,5},{5,9},{9,... | collective-permute-start | bytes 73736 | tf_op jit(solution)/shard_map/ppermute | solution.py:24
  102.4 1.3 collective-permute-start.9
  103.8 3.5 %collective-permute-done.9 = f32[6,2,8,64]{3,2,1,0:T(8,128)S(1)} collective-permute-done((f32[6,2,8,64]{3,2,1,0:T(8,128)S(1)}, f32[6,2,8,64]{3,2,1,0:T(8,128)S(1)}, u32[]{:S(2)}, u32[]{:S(2)}) %collective-permute-start.9) | collective-permute-done | bytes 24608 | tf_op jit(solution)/shard_map/ppermute | solution.py:25
  107.3 3.4 %collective-permute-start.10 = (f32[6,8,2,64]{3,2,1,0:T(2,128)S(1)}, f32[6,8,2,64]{3,2,1,0:T(2,128)S(1)}, u32[]{:S(2)}, u32[]{:S(2)}) collective-permute-start(f32[6,8,2,64]{3,2,1,0:T(2,128)S(1)} %get-tuple-element.168), channel_id=1, source_target_pairs={{0,1},{1,2},{2,3},{4,5},{5,6},{6,7},{8,9},{9,10},{10,11},{12,13},{... | collective-permute-start | bytes 73736 | tf_op jit(solution)/shard_map/ppermute | solution.py:24
  110.7 1.9 %collective-permute-start.11 = (f32[6,8,2,64]{3,2,1,0:T(2,128)S(1)}, f32[6,8,2,64]{3,2,1,0:T(2,128)S(1)}, u32[]{:S(2)}, u32[]{:S(2)}) collective-permute-start(f32[6,8,2,64]{3,2,1,0:T(2,128)S(1)} %get-tuple-element.169), channel_id=1, source_target_pairs={{1,0},{2,1},{3,2},{5,4},{6,5},{7,6},{9,8},{10,9},{11,10},{13,12},{... | collective-permute-start | bytes 73736 | tf_op jit(solution)/shard_map/ppermute | solution.py:25
  112.7 3.4 %collective-permute-done.11 = f32[6,8,2,64]{3,2,1,0:T(2,128)S(1)} collective-permute-done((f32[6,8,2,64]{3,2,1,0:T(2,128)S(1)}, f32[6,8,2,64]{3,2,1,0:T(2,128)S(1)}, u32[]{:S(2)}, u32[]{:S(2)}) %collective-permute-start.11) | collective-permute-done | bytes 24608 | tf_op jit(solution)/shard_map/ppermute | solution.py:25
  117.8 3.1 %collective-permute-start.12 = (f32[6,2,8,64]{3,2,1,0:T(8,128)S(1)}, f32[6,2,8,64]{3,2,1,0:T(8,128)S(1)}, u32[]{:S(2)}, u32[]{:S(2)}) collective-permute-start(f32[6,2,8,64]{3,2,1,0:T(8,128)S(1)} %get-tuple-element.196), channel_id=1, source_target_pairs={{0,4},{4,8},{8,12},{12,16},{16,20},{20,24},{24,28},{1,5},{5,9},{9,... | collective-permute-start | bytes 73736 | tf_op jit(solution)/shard_map/ppermute | solution.py:24
  120.9 1.3 collective-permute-start.13
  122.2 3.5 %collective-permute-done.13 = f32[6,2,8,64]{3,2,1,0:T(8,128)S(1)} collective-permute-done((f32[6,2,8,64]{3,2,1,0:T(8,128)S(1)}, f32[6,2,8,64]{3,2,1,0:T(8,128)S(1)}, u32[]{:S(2)}, u32[]{:S(2)}) %collective-permute-start.13) | collective-permute-done | bytes 24608 | tf_op jit(solution)/shard_map/ppermute | solution.py:25
  125.7 3.3 %collective-permute-start.14 = (f32[6,8,2,64]{3,2,1,0:T(2,128)S(1)}, f32[6,8,2,64]{3,2,1,0:T(2,128)S(1)}, u32[]{:S(2)}, u32[]{:S(2)}) collective-permute-start(f32[6,8,2,64]{3,2,1,0:T(2,128)S(1)} %get-tuple-element.166), channel_id=1, source_target_pairs={{0,1},{1,2},{2,3},{4,5},{5,6},{6,7},{8,9},{9,10},{10,11},{12,13},{... | collective-permute-start | bytes 73736 | tf_op jit(solution)/shard_map/ppermute | solution.py:24
  129.1 1.9 %collective-permute-start.15 = (f32[6,8,2,64]{3,2,1,0:T(2,128)S(1)}, f32[6,8,2,64]{3,2,1,0:T(2,128)S(1)}, u32[]{:S(2)}, u32[]{:S(2)}) collective-permute-start(f32[6,8,2,64]{3,2,1,0:T(2,128)S(1)} %get-tuple-element.167), channel_id=1, source_target_pairs={{1,0},{2,1},{3,2},{5,4},{6,5},{7,6},{9,8},{10,9},{11,10},{13,12},{... | collective-permute-start | bytes 73736 | tf_op jit(solution)/shard_map/ppermute | solution.py:25
  131.0 0.7 reshape.330
  131.7 2.8 %collective-permute-done.15 = f32[6,8,2,64]{3,2,1,0:T(2,128)S(1)} collective-permute-done((f32[6,8,2,64]{3,2,1,0:T(2,128)S(1)}, f32[6,8,2,64]{3,2,1,0:T(2,128)S(1)}, u32[]{:S(2)}, u32[]{:S(2)}) %collective-permute-start.15) | collective-permute-done | bytes 24608 | tf_op jit(solution)/shard_map/ppermute | solution.py:25
  136.1 0.7 reshape.329
  (198 shorter events, 18.5 us)
Async XLA Ops:
  1.5 11.0 %copy-start.5 = (f32[3,4,8,64]{3,2,1,0:T(8,128)}, f32[3,4,8,64]{3,2,1,0:T(8,128)S(1)}, u32[]{:S(2)}) copy-start(f32[3,4,8,64]{3,2,1,0:T(8,128)S(1)} %reshape.316) | copy-start | bytes 73732
  3.0 9.5 %copy-start.7 = (f32[3,4,8,64]{3,2,1,0:T(8,128)}, f32[3,4,8,64]{3,2,1,0:T(8,128)S(1)}, u32[]{:S(2)}) copy-start(f32[3,4,8,64]{3,2,1,0:T(8,128)S(1)} %reshape_squeeze.9) | copy-start | bytes 73732
  3.0 13.7 %collective-permute-start = (f32[6,2,8,64]{3,2,1,0:T(8,128)S(1)}, f32[6,2,8,64]{3,2,1,0:T(8,128)S(1)}, u32[]{:S(2)}, u32[]{:S(2)}) collective-permute-start(f32[6,2,8,64]{3,2,1,0:T(8,128)S(1)} %get-tuple-element.200), channel_id=1, source_target_pairs={{0,4},{4,8},{8,12},{12,16},{16,20},{20,24},{24,28},{1,5},{5,9},{9,... | collective-permute-start | bytes 73736 | tf_op jit(solution)/shard_map/ppermute | solution.py:24
  7.0 9.8 %collective-permute-start.1 = (f32[6,2,8,64]{3,2,1,0:T(8,128)S(1)}, f32[6,2,8,64]{3,2,1,0:T(8,128)S(1)}, u32[]{:S(2)}, u32[]{:S(2)}) collective-permute-start(f32[6,2,8,64]{3,2,1,0:T(8,128)S(1)} %get-tuple-element.201), channel_id=1, source_target_pairs={{4,0},{8,4},{12,8},{16,12},{20,16},{24,20},{28,24},{5,1},{9,5},{13... | collective-permute-start | bytes 73736 | tf_op jit(solution)/shard_map/ppermute | solution.py:25
  8.4 0.5 copy-start.16
  9.3 12.9 %copy-start.13 = (f32[3,32,8,64]{3,2,1,0:T(8,128)S(1)}, f32[3,32,8,64]{3,2,1,0:T(8,128)}, u32[]{:S(2)}) copy-start(f32[3,32,8,64]{3,2,1,0:T(8,128)} %param.18) | copy-start | bytes 589828
  9.3 12.9 %copy-start.14 = (f32[3,32,8,64]{3,2,1,0:T(8,128)S(1)}, f32[3,32,8,64]{3,2,1,0:T(8,128)}, u32[]{:S(2)}) copy-start(f32[3,32,8,64]{3,2,1,0:T(8,128)} %param.19) | copy-start | bytes 589828
  12.5 14.0 %all-to-all-start = ((f32[4,1,6144]{2,1,0:T(1,128)}), f32[4,1,6144]{2,1,0:T(1,128)S(1)}, u32[]{:S(2)}, u32[]{:S(2)}) async-start(f32[4,1,6144]{2,1,0:T(1,128)} %reshape.351), calls=%async_computation | async-start | bytes 196608 | tf_op jit(solution)/shard_map/all_to_all | solution.py:114
  16.7 9.0 %copy-start.1 = (f32[6,2,8,64]{3,2,1,0:T(8,128)}, f32[6,2,8,64]{3,2,1,0:T(8,128)S(1)}, u32[]{:S(2)}) copy-start(f32[6,2,8,64]{3,2,1,0:T(8,128)S(1)} %collective-permute-done) | copy-start | bytes 73732
  16.7 9.0 %copy-start.3 = (f32[6,2,8,64]{3,2,1,0:T(8,128)}, f32[6,2,8,64]{3,2,1,0:T(8,128)S(1)}, u32[]{:S(2)}) copy-start(f32[6,2,8,64]{3,2,1,0:T(8,128)S(1)} %collective-permute-done.1) | copy-start | bytes 73732
  16.8 6.3 %collective-permute-start.2 = (f32[6,8,2,64]{3,2,1,0:T(2,128)S(1)}, f32[6,8,2,64]{3,2,1,0:T(2,128)S(1)}, u32[]{:S(2)}, u32[]{:S(2)}) collective-permute-start(f32[6,8,2,64]{3,2,1,0:T(2,128)S(1)} %get-tuple-element.170), channel_id=1, source_target_pairs={{0,1},{1,2},{2,3},{4,5},{5,6},{6,7},{8,9},{9,10},{10,11},{12,13},{... | collective-permute-start | bytes 73736 | tf_op jit(solution)/shard_map/ppermute | solution.py:24
  20.3 5.4 %collective-permute-start.3 = (f32[6,8,2,64]{3,2,1,0:T(2,128)S(1)}, f32[6,8,2,64]{3,2,1,0:T(2,128)S(1)}, u32[]{:S(2)}, u32[]{:S(2)}) collective-permute-start(f32[6,8,2,64]{3,2,1,0:T(2,128)S(1)} %get-tuple-element.171), channel_id=1, source_target_pairs={{1,0},{2,1},{3,2},{5,4},{6,5},{7,6},{9,8},{10,9},{11,10},{13,12},{... | collective-permute-start | bytes 73736 | tf_op jit(solution)/shard_map/ppermute | solution.py:25
  23.1 2.7 %copy-start.9 = (f32[6,8,2,64]{3,2,1,0:T(2,128)}, f32[6,8,2,64]{3,2,1,0:T(2,128)S(1)}, u32[]{:S(2)}) copy-start(f32[6,8,2,64]{3,2,1,0:T(2,128)S(1)} %collective-permute-done.2) | copy-start | bytes 73732
  25.7 0.6 copy-start.11
  32.6 8.3 %copy-start.2 = (f32[6,2,8,64]{3,2,1,0:T(8,128)S(1)}, f32[6,2,8,64]{3,2,1,0:T(8,128)}, u32[]{:S(2)}) copy-start(f32[6,2,8,64]{3,2,1,0:T(8,128)} %copy-done.1) | copy-start | bytes 73732
  32.6 8.3 %copy-start.4 = (f32[6,2,8,64]{3,2,1,0:T(8,128)S(1)}, f32[6,2,8,64]{3,2,1,0:T(8,128)}, u32[]{:S(2)}) copy-start(f32[6,2,8,64]{3,2,1,0:T(8,128)} %copy-done.3) | copy-start | bytes 73732
  32.6 8.3 %copy-start.10 = (f32[6,8,2,64]{3,2,1,0:T(2,128)S(1)}, f32[6,8,2,64]{3,2,1,0:T(2,128)}, u32[]{:S(2)}) copy-start(f32[6,8,2,64]{3,2,1,0:T(2,128)} %copy-done.9) | copy-start | bytes 73732
  32.6 8.3 %copy-start.12 = (f32[6,8,2,64]{3,2,1,0:T(2,128)S(1)}, f32[6,8,2,64]{3,2,1,0:T(2,128)}, u32[]{:S(2)}) copy-start(f32[6,8,2,64]{3,2,1,0:T(2,128)} %copy-done.11) | copy-start | bytes 73732
  34.2 13.4 %all-to-all-start.1 = ((f32[8,1,6144]{2,1,0:T(1,128)}), f32[8,1,6144]{2,1,0:T(1,128)S(1)}, u32[]{:S(2)}, u32[]{:S(2)}) async-start(f32[8,1,6144]{2,1,0:T(1,128)} %reshape.353), calls=%async_computation.1 | async-start | bytes 393216 | tf_op jit(solution)/shard_map/all_to_all | solution.py:126
  50.3 1.6 %copy-start = (f32[1,32,8,64]{3,2,1,0:T(8,128)S(1)}, f32[1,32,8,64]{3,2,1,0:T(8,128)}, u32[]{:S(2)}) copy-start(f32[1,32,8,64]{3,2,1,0:T(8,128)} %get-tuple-element.213) | copy-start | bytes 196612
  56.0 11.0 %all-to-all-start.2 = ((f32[8,1,6144]{2,1,0:T(1,128)}), f32[8,1,6144]{2,1,0:T(1,128)S(1)}, u32[]{:S(2)}, u32[]{:S(2)}) async-start(f32[8,1,6144]{2,1,0:T(1,128)} %reshape.355), calls=%async_computation.2 | async-start | bytes 393216 | tf_op jit(solution)/shard_map/all_to_all | solution.py:160
  71.4 7.9 %all-to-all-start.3 = ((f32[4,1,6144]{2,1,0:T(1,128)}), f32[4,1,6144]{2,1,0:T(1,128)S(1)}, u32[]{:S(2)}, u32[]{:S(2)}) async-start(f32[4,1,6144]{2,1,0:T(1,128)} %reshape.357), calls=%async_computation.3 | async-start | bytes 196608 | tf_op jit(solution)/shard_map/all_to_all | solution.py:172
  76.0 4.9 %copy-start.17 = (s32[128]{0:T(128)S(1)}, s32[128]{0:T(128)}, u32[]{:S(2)}) copy-start(s32[128]{0:T(128)} %copy-done.16) | copy-start | bytes 1540
  81.7 4.0 %collective-permute-start.4 = (f32[3,1,8,64]{3,2,1,0:T(8,128)S(1)}, f32[3,1,8,64]{3,2,1,0:T(8,128)S(1)}, u32[]{:S(2)}, u32[]{:S(2)}) collective-permute-start(f32[3,1,8,64]{3,2,1,0:T(8,128)S(1)} %get-tuple-element.207), channel_id=1, source_target_pairs={{0,4},{4,8},{8,12},{12,16},{16,20},{20,24},{24,28},{1,5},{5,9},{9,... | collective-permute-start | bytes 18440 | tf_op jit(solution)/shard_map/ppermute | solution.py:24
  84.3 4.4 %collective-permute-start.5 = (f32[3,1,8,64]{3,2,1,0:T(8,128)S(1)}, f32[3,1,8,64]{3,2,1,0:T(8,128)S(1)}, u32[]{:S(2)}, u32[]{:S(2)}) collective-permute-start(f32[3,1,8,64]{3,2,1,0:T(8,128)S(1)} %get-tuple-element.208), channel_id=1, source_target_pairs={{4,0},{8,4},{12,8},{16,12},{20,16},{24,20},{28,24},{5,1},{9,5},{13... | collective-permute-start | bytes 18440 | tf_op jit(solution)/shard_map/ppermute | solution.py:25
  88.8 6.5 %collective-permute-start.6 = (f32[3,6,1,64]{3,2,1,0:T(1,128)S(1)}, f32[3,6,1,64]{3,2,1,0:T(1,128)S(1)}, u32[]{:S(2)}, u32[]{:S(2)}) collective-permute-start(f32[3,6,1,64]{3,2,1,0:T(1,128)S(1)} %get-tuple-element.205), channel_id=1, source_target_pairs={{0,1},{1,2},{2,3},{4,5},{5,6},{6,7},{8,9},{9,10},{10,11},{12,13},{... | collective-permute-start | bytes 13832 | tf_op jit(solution)/shard_map/ppermute | solution.py:24
  93.2 5.0 %collective-permute-start.7 = (f32[3,6,1,64]{3,2,1,0:T(1,128)S(1)}, f32[3,6,1,64]{3,2,1,0:T(1,128)S(1)}, u32[]{:S(2)}, u32[]{:S(2)}) collective-permute-start(f32[3,6,1,64]{3,2,1,0:T(1,128)S(1)} %get-tuple-element.206), channel_id=1, source_target_pairs={{1,0},{2,1},{3,2},{5,4},{6,5},{7,6},{9,8},{10,9},{11,10},{13,12},{... | collective-permute-start | bytes 13832 | tf_op jit(solution)/shard_map/ppermute | solution.py:25
  98.4 0.8 copy-start.8
  98.5 0.9 copy-start.6
  98.6 14.0 %copy-start.15 = (f32[1,3,4,512]{3,2,1,0:T(4,128)S(1)}, f32[1,3,4,512]{3,2,1,0:T(4,128)}, u32[]{:S(2)}) copy-start(f32[1,3,4,512]{3,2,1,0:T(4,128)} %get-tuple-element.202) | copy-start | bytes 73732
  99.5 4.3 %collective-permute-start.8 = (f32[6,2,8,64]{3,2,1,0:T(8,128)S(1)}, f32[6,2,8,64]{3,2,1,0:T(8,128)S(1)}, u32[]{:S(2)}, u32[]{:S(2)}) collective-permute-start(f32[6,2,8,64]{3,2,1,0:T(8,128)S(1)} %get-tuple-element.198), channel_id=1, source_target_pairs={{0,4},{4,8},{8,12},{12,16},{16,20},{20,24},{24,28},{1,5},{5,9},{9,... | collective-permute-start | bytes 73736 | tf_op jit(solution)/shard_map/ppermute | solution.py:24
  102.4 4.8 %collective-permute-start.9 = (f32[6,2,8,64]{3,2,1,0:T(8,128)S(1)}, f32[6,2,8,64]{3,2,1,0:T(8,128)S(1)}, u32[]{:S(2)}, u32[]{:S(2)}) collective-permute-start(f32[6,2,8,64]{3,2,1,0:T(8,128)S(1)} %get-tuple-element.199), channel_id=1, source_target_pairs={{4,0},{8,4},{12,8},{16,12},{20,16},{24,20},{28,24},{5,1},{9,5},{13... | collective-permute-start | bytes 73736 | tf_op jit(solution)/shard_map/ppermute | solution.py:25
  107.3 5.4 %collective-permute-start.10 = (f32[6,8,2,64]{3,2,1,0:T(2,128)S(1)}, f32[6,8,2,64]{3,2,1,0:T(2,128)S(1)}, u32[]{:S(2)}, u32[]{:S(2)}) collective-permute-start(f32[6,8,2,64]{3,2,1,0:T(2,128)S(1)} %get-tuple-element.168), channel_id=1, source_target_pairs={{0,1},{1,2},{2,3},{4,5},{5,6},{6,7},{8,9},{9,10},{10,11},{12,13},{... | collective-permute-start | bytes 73736 | tf_op jit(solution)/shard_map/ppermute | solution.py:24
  110.7 5.4 %collective-permute-start.11 = (f32[6,8,2,64]{3,2,1,0:T(2,128)S(1)}, f32[6,8,2,64]{3,2,1,0:T(2,128)S(1)}, u32[]{:S(2)}, u32[]{:S(2)}) collective-permute-start(f32[6,8,2,64]{3,2,1,0:T(2,128)S(1)} %get-tuple-element.169), channel_id=1, source_target_pairs={{1,0},{2,1},{3,2},{5,4},{6,5},{7,6},{9,8},{10,9},{11,10},{13,12},{... | collective-permute-start | bytes 73736 | tf_op jit(solution)/shard_map/ppermute | solution.py:25
  117.8 4.4 %collective-permute-start.12 = (f32[6,2,8,64]{3,2,1,0:T(8,128)S(1)}, f32[6,2,8,64]{3,2,1,0:T(8,128)S(1)}, u32[]{:S(2)}, u32[]{:S(2)}) collective-permute-start(f32[6,2,8,64]{3,2,1,0:T(8,128)S(1)} %get-tuple-element.196), channel_id=1, source_target_pairs={{0,4},{4,8},{8,12},{12,16},{16,20},{20,24},{24,28},{1,5},{5,9},{9,... | collective-permute-start | bytes 73736 | tf_op jit(solution)/shard_map/ppermute | solution.py:24
  120.9 4.8 %collective-permute-start.13 = (f32[6,2,8,64]{3,2,1,0:T(8,128)S(1)}, f32[6,2,8,64]{3,2,1,0:T(8,128)S(1)}, u32[]{:S(2)}, u32[]{:S(2)}) collective-permute-start(f32[6,2,8,64]{3,2,1,0:T(8,128)S(1)} %get-tuple-element.197), channel_id=1, source_target_pairs={{4,0},{8,4},{12,8},{16,12},{20,16},{24,20},{28,24},{5,1},{9,5},{13... | collective-permute-start | bytes 73736 | tf_op jit(solution)/shard_map/ppermute | solution.py:25
  125.7 6.0 %collective-permute-start.14 = (f32[6,8,2,64]{3,2,1,0:T(2,128)S(1)}, f32[6,8,2,64]{3,2,1,0:T(2,128)S(1)}, u32[]{:S(2)}, u32[]{:S(2)}) collective-permute-start(f32[6,8,2,64]{3,2,1,0:T(2,128)S(1)} %get-tuple-element.166), channel_id=1, source_target_pairs={{0,1},{1,2},{2,3},{4,5},{5,6},{6,7},{8,9},{9,10},{10,11},{12,13},{... | collective-permute-start | bytes 73736 | tf_op jit(solution)/shard_map/ppermute | solution.py:24
  129.1 5.4 %collective-permute-start.15 = (f32[6,8,2,64]{3,2,1,0:T(2,128)S(1)}, f32[6,8,2,64]{3,2,1,0:T(2,128)S(1)}, u32[]{:S(2)}, u32[]{:S(2)}) collective-permute-start(f32[6,8,2,64]{3,2,1,0:T(2,128)S(1)} %get-tuple-element.167), channel_id=1, source_target_pairs={{1,0},{2,1},{3,2},{5,4},{6,5},{7,6},{9,8},{10,9},{11,10},{13,12},{... | collective-permute-start | bytes 73736 | tf_op jit(solution)/shard_map/ppermute | solution.py:25
where the time goes:
time: 138 us; the launch traced here: 137 us
  starting transfers between devices  59 us (43%)
  waiting for transfers between devices  39.1 us (28%)
  local copies, waits for them, and re-layouts  19.8 us (14%)
  matrix products  9.29 us (7%)
  other arithmetic  7.76 us (6%)
  between operations  1.96 us (1%)
    ppermute x8, starting transfers between devices, with_halo(): before = lax.ppermute(last, axis, up)  27.3 us
    ppermute x8, waiting for transfers between devices, with_halo(): after = lax.ppermute(first, axis, down)  21.8 us
    ppermute x8, starting transfers between devices, with_halo(): after = lax.ppermute(first, axis, down)  12.9 us
    unnamed x45, local copies, waits for them, and re-layouts  9.53 us
    dot_general x20, matrix products, contract(): jnp.einsum(form, data, table, precision=lax.Precision.HIGHEST, preferred_...  9.29 us
    all_to_all x1, waiting for transfers between devices, demagnetize(): lax.all_to_all(jnp.stack([back_real, back_imag]), 'gx', split_axis=4, con...  7.38 us
    all_to_all x1, starting transfers between devices, demagnetize(): lax.all_to_all(jnp.stack([y_real, y_imag]), 'gx', split_axis=3, concat_ax...  6.68 us
    all_to_all x1, waiting for transfers between devices, demagnetize(): lax.all_to_all(jnp.stack([y_real, y_imag]), 'gx', split_axis=3, concat_ax...  6.56 us
  transfers between devices with their start and end apart: 20, of which 10 were waited for; matrix products, arithmetic and copies ran while one was open for 5% of the time, Pallas kernels for 0%

commit v1 on v0

v1 whole, which is shorter than its diff:
```python
import functools

import jax
import jax.numpy as jnp
import ml_dtypes
import numpy as np
from jax import lax
from jax.experimental import pallas as pl
from jax.experimental.pallas import tpu as pltpu
from jax.sharding import PartitionSpec as P

NZ = 64
STEPS = 3
DAMPING = 0.1
TIME_STEP = 0.05
ANISOTROPY = 0.5
LX = 4
LY = 8
MESH = pl.DeviceIdType.MESH
OFFSETS = [(dx, dy) for dx in (-2, -1, 0, 1, 2) for dy in (-1, 0, 1) if (dx, dy) != (0, 0)]
PLACE = {-2: (0, 1, 1), -1: (1, 0, 2), 0: (3, 0, 2), 1: (5, 0, 2), 2: (7, 0, 1)}


def halves(table):
    table = np.asarray(table, np.float32)
    high = table.astype(ml_dtypes.bfloat16)
    low = (table - high.astype(np.float32)).astype(ml_dtypes.bfloat16)
    return np.stack([high, low])


def angles(first, second, period):
    return 2.0 * np.pi * ((np.asarray(first)[:, None] * np.asarray(second)[None, :]) % period) / period


def tables(nx, ny):
    x_all, y_all = nx * LX, ny * LY
    block = 2 * NZ // ny
    kept = block // 2 + 1
    ang = angles(np.arange(2 * y_all), np.arange(y_all), 2 * y_all)
    y_fwd = np.concatenate([np.cos(ang), -np.sin(ang)])
    z_fwd = np.zeros((ny, 3, 2, NZ, 128))
    z_inv = np.zeros((ny, 128, 3, 2, NZ))
    for g in range(ny):
        kz = g * block + np.arange(kept)
        ang = angles(np.arange(NZ), kz, 2 * NZ)
        weight = np.full((kept,), 2.0)
        if g in (0, ny // 2):
            weight[0] = 1.0
        if g > ny // 2:
            weight[0] = 0.0
        if g < ny // 2:
            weight[kept - 1] = 0.0
        weight = -weight / (8.0 * x_all * y_all * NZ)
        for c in range(3):
            re = slice(c * kept, (c + 1) * kept)
            im = slice(64 + c * kept, 64 + (c + 1) * kept)
            z_fwd[g, c, 0, :, re] = np.cos(ang)
            z_fwd[g, c, 1, :, re] = np.sin(ang)
            z_fwd[g, c, 1, :, im] = np.cos(ang)
            z_fwd[g, c, 0, :, im] = -np.sin(ang)
            for copy in range(2):
                z_inv[g, re, c, copy] = (np.cos(ang) * weight).T
                z_inv[g, im, c, copy] = (-np.sin(ang) * weight).T
    z_fwd = z_fwd.reshape(ny, 3 * 2 * NZ, 128)
    z_inv = z_inv.reshape(ny * 128, 3 * 128)
    ang = angles(np.arange(2 * x_all), np.arange(x_all), 2 * x_all)
    eye = np.eye(8)
    x_fwd = np.stack([np.cos(ang), np.sin(ang)])
    x_inv = np.einsum("skx,ab->sxabk", x_fwd, eye).reshape(2 * x_all * 8, 8 * 2 * x_all)
    x_fwd = np.einsum("skx,ab->sakxb", x_fwd, eye).reshape(2 * 8 * 2 * x_all, x_all * 8)
    ang = angles(np.arange(y_all), np.arange(2 * y_all), 2 * y_all)
    y_inv = np.concatenate([np.cos(ang), np.sin(ang)])
    place = np.zeros((3, 2, 3, block, 128))
    pairs = {(0, 1): 0, (0, 2): 1, (1, 2): 2}
    for c in range(3):
        for d in range(3):
            other = (c + d) % 3
            entry = c if d == 0 else pairs[(min(c, other), max(c, other))]
            for half in range(2):
                for j in range(kept):
                    place[d, :, entry, j, half * 64 + c * kept + j] = 1.0
    place = place.reshape(3, 6 * block, 128)
    place = np.concatenate([place[0], place[1], place[2]], axis=1).astype(ml_dtypes.bfloat16)
    return (
        halves(y_fwd),
        np.moveaxis(halves(z_fwd), 0, 1),
        halves(x_fwd),
        halves(x_inv),
        halves(y_inv),
        halves(z_inv),
        place,
    )


def split(value):
    high = value.astype(jnp.bfloat16)
    low = (value - high.astype(jnp.float32)).astype(jnp.bfloat16)
    return high, low


def dot(left, right):
    return jnp.dot(left, right, preferred_element_type=jnp.float32)


def dot_left(table, data):
    high, low = split(data)
    return dot(table[0], high) + (dot(table[0], low) + dot(table[1], high))


def dot_right(data, table):
    high, low = split(data)
    return dot(high, table[0]) + (dot(low, table[0]) + dot(high, table[1]))


def cross(a, b):
    return [a[1] * b[2] - a[2] * b[1], a[2] * b[0] - a[0] * b[2], a[0] * b[1] - a[1] * b[0]]


def kernel(
    nx, ny,
    fields, diag_h, off_h, y_fwd_h, z_fwd_h, x_fwd_h, x_inv_h, y_inv_h, z_inv_h, place_h,
    final_ref, demag_ref,
    diag, off, y_fwd, z_small, z_fwd, x_fwd, x_inv, y_inv, z_inv, place,
    wide, wide_demag, rows_in, spec_out, spec_in, back_out, back_in, row_out, row_in, tensor,
    local_sem, halo_send, halo_recv, dem_send, dem_recv, ag_send, ag_recv,
    fwd_send, fwd_recv, inv_send, inv_recv, last_send, last_recv,
):
    x_all, y_all = nx * LX, ny * LY
    block = 2 * NZ // ny
    kept = block // 2 + 1
    me_x, me_y = lax.axis_index("gx"), lax.axis_index("gy")

    loads = [
        pltpu.make_async_copy(src, dst, local_sem.at[i])
        for i, (src, dst) in enumerate([
            (y_fwd_h, y_fwd), (z_fwd_h.at[me_y], z_small), (diag_h, diag), (off_h, off),
            (place_h, place), (x_fwd_h, x_fwd), (x_inv_h, x_inv), (y_inv_h, y_inv), (z_inv_h, z_inv),
        ])
    ]
    for load in loads:
        load.start()

    def present(dx, dy):
        x, y = me_x + dx, me_y + dy
        return (x >= 0) & (x < nx) & (y >= 0) & (y < ny)

    barrier = pltpu.get_barrier_semaphore()
    diagonal = [(dx, dy) for dx, dy in OFFSETS if dx and dy]
    for i in range(1, nx):
        pl.semaphore_signal(barrier, 1, device_id=(lax.rem(me_x + i, nx), me_y), device_id_type=MESH)
    for i in range(1, ny):
        pl.semaphore_signal(barrier, 1, device_id=(me_x, lax.rem(me_y + i, ny)), device_id_type=MESH)
    for dx, dy in diagonal:
        @pl.when(present(dx, dy))
        def _():
            pl.semaphore_signal(barrier, 1, device_id=(me_x + dx, me_y + dy), device_id_type=MESH)
    beside_x = jnp.minimum(me_x, 2) + jnp.minimum(nx - 1 - me_x, 2)
    beside_y = jnp.minimum(me_y, 1) + jnp.minimum(ny - 1 - me_y, 1)
    pl.semaphore_wait(barrier, nx + ny - 2 + beside_x * beside_y)

    def along_y(i, src, dst, send, recv):
        return pltpu.make_async_remote_copy(
            src, dst, send.at[i], recv.at[i],
            device_id=(me_x, lax.rem(me_y + i, ny)), device_id_type=MESH)

    def along_x(i, src, dst, send, recv):
        return pltpu.make_async_remote_copy(
            src, dst, send.at[i], recv.at[i],
            device_id=(lax.rem(me_x + i, nx), me_y), device_id_type=MESH)

    gather = [along_y(i, fields.at[0], rows_in.at[me_y], ag_send, ag_recv) for i in range(1, ny)]
    for copy in gather:
        copy.start()

    def halo(i, kind):
        dx, dy = OFFSETS[i]
        at, first, count = PLACE[-dx]
        if kind == 0:
            many = 2 if abs(dx) == 2 else 4
            src = fields.at[pl.ds(0, many), :, pl.ds(first, count)]
            dst = wide.at[pl.ds(0, many), :, pl.ds(at, count), 1 - dy]
            send, recv = halo_send, halo_recv
        else:
            src = demag_ref.at[:, pl.ds(first, count)]
            dst = wide_demag.at[:, pl.ds(at, count), 1 - dy]
            send, recv = dem_send, dem_recv
        return pltpu.make_async_remote_copy(
            src, dst, send.at[i], recv.at[i],
            device_id=(me_x + dx, me_y + dy), device_id_type=MESH)

    def halo_start(kind):
        for i, (dx, dy) in enumerate(OFFSETS):
            @pl.when(present(dx, dy))
            def _():
                halo(i, kind).start()

    def halo_wait(kind):
        for i, (dx, dy) in enumerate(OFFSETS):
            @pl.when(present(dx, dy))
            def _():
                halo(i, kind).wait_send()

            @pl.when(present(-dx, -dy))
            def _():
                halo(i, kind).wait_recv()

    halo_start(0)
    wide[0:4, :, 3:5, 1] = fields[...]
    rows_in[me_y] = fields[0]

    for i in (2, 3, 4):
        loads[i].wait()
    for y in range(8):
        for source, first, last in ((diag, 0, 128), (off, 128, 384)):
            piece = source[:, :, y, :].reshape(3 * block, 2 * x_all)
            high, low = split(piece)
            both = jnp.concatenate([high, low], axis=0)
            tensor[pl.ds(y * 2 * x_all, 2 * x_all), first:last] = lax.dot_general(
                both, place[:, first:last], (((0,), (0,)), ((), ())), preferred_element_type=jnp.float32)

    loads[1].wait()
    z_fwd[...] = jnp.zeros_like(z_fwd)
    for x in range(2):
        for part in range(6):
            z_fwd[:, pl.ds(128 * part + NZ * x, NZ), 128 * x : 128 * (x + 1)] = z_small[:, pl.ds(NZ * part, NZ)]
    loads[0].wait()
    for copy in gather:
        copy.wait()
    data = jnp.concatenate(
        [rows_in[:, c, t].reshape(y_all, 128) for c in range(3) for t in range(2)], axis=1)
    spectrum = dot_left(y_fwd, data)
    for t in range(2):
        parts = []
        for c in range(3):
            lanes = slice((2 * c + t) * 128, (2 * c + t + 1) * 128)
            parts += [spectrum[: 2 * y_all, lanes], spectrum[2 * y_all :, lanes]]
        planes = dot_right(jnp.concatenate(parts, axis=1), z_fwd)
        for x in range(2):
            spec_out[:, 2 * t + x] = planes[:, x * 128 : (x + 1) * 128].reshape(nx, 8, 128)
    forward = [
        along_x(i, spec_out.at[lax.rem(me_x + i, nx)], spec_in.at[me_x], fwd_send, fwd_recv)
        for i in range(1, nx)
    ]
    for copy in forward:
        copy.start()
    spec_in[me_x] = spec_out[me_x]
    loads[5].wait()
    loads[6].wait()
    lane = lax.broadcasted_iota(jnp.int32, (1, 128), 1)
    low_half = lane < 64
    component = lax.rem(lane, 64)
    turn = jnp.where(low_half, 1.0, -1.0).astype(jnp.float32)
    for copy in forward:
        copy.wait()

    size = 8 * 2 * x_all
    both = dot_left(x_fwd, spec_in[...].reshape(x_all * 8, 128))
    spectra = both[:size] + turn * pltpu.roll(both[size:], 64, 1)
    second = jnp.where(component < 2 * kept, pltpu.roll(spectra, 128 - kept, 1), pltpu.roll(spectra, 2 * kept, 1))
    third = jnp.where(component < kept, pltpu.roll(spectra, 128 - 2 * kept, 1), pltpu.roll(spectra, kept, 1))
    response = tensor[:, :128] * spectra + tensor[:, 128:256] * second + tensor[:, 256:] * third
    both = dot_left(x_inv, response)
    back = both[: x_all * 8] - turn * pltpu.roll(both[x_all * 8 :], 64, 1)
    back_out[...] = back.reshape(nx, LX, 8, 128)
    inverse = [
        along_x(i, back_out.at[lax.rem(me_x + i, nx)], back_in.at[me_x], inv_send, inv_recv)
        for i in range(1, nx)
    ]
    for copy in inverse:
        copy.start()
    back_in[me_x] = back_out[me_x]
    loads[7].wait()
    loads[8].wait()
    for copy in inverse:
        copy.wait()
    data = jnp.concatenate([back_in[:, x].reshape(nx * 8, 128) for x in range(LX)], axis=1)
    both = dot_left(y_inv, data)
    for x in range(LX):
        lanes = slice(x * 128, (x + 1) * 128)
        rows = both[:y_all, lanes] - turn * pltpu.roll(both[y_all:, lanes], 64, 1)
        row_out[:, x] = rows.reshape(ny, LY, 128)
    final = [
        along_y(i, row_out.at[lax.rem(me_y + i, ny)], row_in.at[me_y], last_send, last_recv)
        for i in range(1, ny)
    ]
    for copy in final:
        copy.start()
    row_in[me_y] = row_out[me_y]
    for copy in final:
        copy.wait()
    data = jnp.concatenate([row_in[g].reshape(LX * LY, 128) for g in range(ny)], axis=1)
    rows = dot_right(data, z_inv)
    for c in range(3):
        lanes = slice(c * 128, (c + 1) * 128)
        for t in range(2):
            demag_ref[c, t] = jnp.where(
                low_half, rows[16 * t : 16 * t + 8, lanes], rows[16 * t + 8 : 16 * t + 16, lanes])
    halo_start(1)
    wide_demag[:, 3:5, 1] = demag_ref[...]
    halo_wait(0)
    halo_wait(1)

    shape = (8, 3 * LY, 128)
    lanes = lax.broadcasted_iota(jnp.int32, shape, 2)
    x_at = LX * me_x - 6 + 2 * lax.broadcasted_iota(jnp.int32, shape, 0) + lanes // 64
    y_at = LY * me_y - LY + lax.broadcasted_iota(jnp.int32, shape, 1)
    z_at = lax.rem(lanes, 64)
    left_half = lanes < 64
    at_x0, at_x1 = x_at == 0, x_at == x_all - 1
    at_y0, at_y1 = y_at == 0, y_at == y_all - 1
    at_z0, at_z1 = z_at == 0, z_at == NZ - 1

    def laplace(v):
        turned = pltpu.roll(v, 64, 2)
        up = jnp.where(left_half, turned, jnp.concatenate([turned[1:], turned[-1:]], axis=0))
        down = jnp.where(left_half, jnp.concatenate([turned[:1], turned[:-1]], axis=0), turned)
        total = jnp.where(at_x1, v, up) + jnp.where(at_x0, v, down)
        total = total + jnp.where(at_y1, v, pltpu.roll(v, 3 * LY - 1, 1))
        total = total + jnp.where(at_y0, v, pltpu.roll(v, 1, 1))
        total = total + jnp.where(at_z1, v, pltpu.roll(v, 127, 2))
        total = total + jnp.where(at_z0, v, pltpu.roll(v, 1, 2))
        return total - 6.0 * v

    def torque(v, noise):
        h = [laplace(v[c]) + noise[c] for c in range(3)]
        h[2] = h[2] + ANISOTROPY * v[2]
        first = cross(v, h)
        second = cross(v, first)
        return [(first[c] + DAMPING * second[c]) * (-1.0 / (1.0 + DAMPING * DAMPING)) for c in range(3)]

    m = [wide[0, c].reshape(shape) for c in range(3)]
    for s in range(STEPS):
        noise = [wide_demag[c].reshape(shape) + wide[1 + s, c].reshape(shape) for c in range(3)]
        f0 = torque(m, noise)
        f1 = torque([m[c] + TIME_STEP * f0[c] for c in range(3)], noise)
        u = [m[c] + 0.5 * TIME_STEP * (f0[c] + f1[c]) for c in range(3)]
        norm = jnp.sqrt(u[0] * u[0] + u[1] * u[1] + u[2] * u[2])
        m = [u[c] / norm for c in range(3)]
    for c in range(3):
        final_ref[c] = m[c][3:5, LY : 2 * LY]


def body(nx, ny, magnet, thermal, kernel_diag, kernel_off):
    block = 2 * NZ // ny
    x_all, y_all = nx * LX, ny * LY
    consts = tables(nx, ny)
    fields = jnp.concatenate([magnet[None], thermal])
    fields = fields.reshape(1 + STEPS, 3, LX // 2, 2, LY, NZ)
    fields = jnp.swapaxes(fields, 3, 4).reshape(1 + STEPS, 3, LX // 2, LY, 2 * NZ)
    vmem = pl.BlockSpec(memory_space=pltpu.VMEM)
    anyspace = pl.BlockSpec(memory_space=pl.ANY)
    out = jax.ShapeDtypeStruct((3, LX // 2, LY, 2 * NZ), jnp.float32)
    f32, bf16 = jnp.float32, jnp.bfloat16
    scratch = [
        pltpu.VMEM(kernel_diag.shape, f32),
        pltpu.VMEM(kernel_off.shape, f32),
        pltpu.VMEM(consts[0].shape, bf16),
        pltpu.VMEM(consts[1].shape[1:], bf16),
        pltpu.VMEM((2, 3 * 2 * 2 * NZ, 256), bf16),
        *[pltpu.VMEM(c.shape, bf16) for c in consts[2:]],
        pltpu.VMEM((1 + STEPS, 3, 8, 3, LY, 128), f32),
        pltpu.VMEM((3, 8, 3, LY, 128), f32),
        pltpu.VMEM((ny, 3, 2, LY, 128), f32),
        *[pltpu.VMEM((nx, LX, 8, 128), f32)] * 4,
        *[pltpu.VMEM((ny, LX, LY, 128), f32)] * 2,
        pltpu.VMEM((8 * 2 * x_all, 384), f32),
        pltpu.SemaphoreType.DMA((9,)),
        *[pltpu.SemaphoreType.DMA((len(OFFSETS),))] * 4,
        *[pltpu.SemaphoreType.DMA((ny,))] * 2,
        *[pltpu.SemaphoreType.DMA((nx,))] * 4,
        *[pltpu.SemaphoreType.DMA((ny,))] * 2,
    ]
    final, demag = pl.pallas_call(
        functools.partial(kernel, nx, ny),
        out_shape=(out, out),
        in_specs=[vmem] + [anyspace] * 9,
        out_specs=(vmem, vmem),
        scratch_shapes=scratch,
        compiler_params=pltpu.CompilerParams(
            collective_id=0, has_side_effects=True, vmem_limit_bytes=56 * 1024 * 1024),
    )(fields, kernel_diag, kernel_off, *[jnp.asarray(c) for c in consts])

    def natural(value):
        value = value.reshape(3, LX // 2, LY, 2, NZ)
        return jnp.swapaxes(value, 2, 3).reshape(3, LX, LY * NZ)

    return natural(final), natural(demag)


def solution(mesh):
    in_specs = (
        P(None, "gx", "gy"),
        P(None, None, "gx", "gy"),
        P(None, "gy", "gx", None),
        P(None, "gy", "gx", None),
    )
    out_specs = (P(None, "gx", "gy"), P(None, "gx", "gy"))
    run = functools.partial(body, mesh.shape["gx"], mesh.shape["gy"])
    return jax.shard_map(run, mesh=mesh, in_specs=in_specs, out_specs=out_specs, check_vma=False)
```

time: 138 us -> 41.6 us (0.30)
  starting transfers between devices: 59 us -> 0 us
  waiting for transfers between devices: 39.1 us -> 0 us
  Pallas kernels: 0 us -> 36.2 us
  local copies, waits for them, and re-layouts: 19.8 us -> 4.21 us
  matrix products: 9.29 us -> 0 us
  other arithmetic: 7.76 us -> 0.1 us
    ppermute x16 -> x0, starting transfers between devices: 40.1 us -> none  [the longest x8 27.3 us: with_halo(): before = lax.ppermute(last, axis, up)]
    pallas_call x0 -> x1, Pallas kernels: none -> 36.2 us  [body(): pl.pallas_call(functools.partial(kernel, nx, ny), out_shape=(out, out), i...]
    ppermute x16 -> x0, waiting for transfers between devices: 21.9 us -> none  [the longest x8 21.8 us: with_halo(): after = lax.ppermute(first, axis, down)]
    all_to_all x4 -> x0, starting transfers between devices: 18.8 us -> none  [the longest x1 6.68 us: demagnetize(): lax.all_to_all(jnp.stack([y_real, y_imag]), 'gx', split_axis=3, concat_ax...]
    all_to_all x4 -> x0, waiting for transfers between devices: 17.2 us -> none  [the longest x1 7.38 us: demagnetize(): lax.all_to_all(jnp.stack([back_real, back_imag]), 'gx', split_axis=4, con...]
    unnamed x45 -> x4, local copies, waits for them, and re-layouts: 9.53 us -> 0.04 us
    dot_general x20 -> x0, matrix products: 9.29 us -> none  [contract(): jnp.einsum(form, data, table, precision=lax.Precision.HIGHEST, preferred_...]
    all_to_all x4 -> x0, other arithmetic: 4 us -> none  [the longest x1 1.1 us: demagnetize(): lax.all_to_all(jnp.stack([y_real, y_imag]), 'gx', split_axis=3, concat_ax...]
  transfers between devices with their start and end apart: 20 -> 0, of which waited for: 10 -> 0; matrix products, arithmetic and copies ran while one was open for 5% -> 0% of each run, Pallas kernels for 0% -> 0%
where the time goes in v1:
time: 41.6 us; the launch traced here: 41.2 us
  Pallas kernels  36.2 us (87%)
  local copies, waits for them, and re-layouts  4.21 us (10%)
  between operations  0.71 us (2%)
    pallas_call x1, Pallas kernels, body(): pl.pallas_call(functools.partial(kernel, nx, ny), out_shape=(out, out), i...  36.2 us
    reshape x2, local copies, waits for them, and re-layouts, natural(): return jnp.swapaxes(value, 2, 3).reshape(3, LX, LY * NZ)  1.38 us
    concatenate x4, local copies, waits for them, and re-layouts, body(): fields = jnp.concatenate([magnet[None], thermal])  1.07 us
    reshape x2, local copies, waits for them, and re-layouts, natural(): value = value.reshape(3, LX // 2, LY, 2, NZ)  0.92 us

profile of v1, /device:TPU:1, one launch (start us, length us, event | category | flops | bytes accessed | tf_op | source)
XLA Modules:
  0.0 41.2 jit_solution(14098349078442552913)
XLA Ops:
  0.6 0.0 copy-start
  0.6 0.9 %concatenate.8 = f32[1,3,2,2,8,64]{5,4,3,2,1,0:T(8,128)S(1)} reshape(f32[3,4,512]{2,1,0:T(4,128)} %param.11) | data formatting | bytes 49152 | tf_op jit(solution)/shard_map/concatenate | solution.py:347
  1.5 0.0 copy-done
  1.5 0.1 concatenate.9
  1.6 0.1 copy.14
  1.7 0.1 maximum_bitcast_fusion
  1.8 0.8 %reshape.23.fields = f32[4,3,2,8,128]{4,3,2,1,0:T(8,128)} reshape(f32[4,3,2,8,2,64]{5,4,3,2,1,0:T(2,128)S(1)} %maximum_bitcast_fusion) | data formatting | bytes 196608 | tf_op jit(solution)/shard_map/reshape | solution.py:349
  2.6 36.2 %shard_map.122 = (f32[3,2,8,128]{3,2,1,0:T(8,128)}, f32[3,2,8,128]{3,2,1,0:T(8,128)}) custom-call(f32[4,3,2,8,128]{4,3,2,1,0:T(8,128)} %reshape.23.fields, f32[3,32,8,64]{3,2,1,0:T(8,128)} %diag_h.1, f32[3,32,8,64]{3,2,1,0:T(8,128)} %off_h.1, bf16[2,128,32]{2,1,0:T(8,128)(2,1)} %constant.14.clone.y_fwd_h, bf16[4,2,384,128]{3,2,1,0:T(8,128)(2,1)} %constant.15.clone.z_fwd_h, ...), custom_call_target="tpu_custom_call" | custom-call | tf_op jit(solution)/shard_map/pallas_call | solution.py:373
  38.9 0.8 %reshape.24 = f32[3,2,8,2,64]{4,3,2,1,0:T(2,128)S(1)} reshape(f32[3,2,8,128]{3,2,1,0:T(8,128)} %get-tuple-element.4) | data formatting | bytes 49152 | tf_op jit(solution)/shard_map/reshape | solution.py:384
  39.7 0.0 copy-start.1
  39.7 0.7 %reshape.25 = f32[3,4,512]{2,1,0:T(4,128)} reshape(f32[3,2,2,8,64]{4,3,2,1,0:T(8,128)S(1)} %copy.15) | data formatting | bytes 49152 | tf_op jit(solution)/shard_map/reshape | solution.py:385
  40.4 0.0 copy-done.1
  40.4 0.1 reshape.26
  40.6 0.7 %reshape.27 = f32[3,4,512]{2,1,0:T(4,128)} reshape(f32[3,2,2,8,64]{4,3,2,1,0:T(8,128)S(1)} %copy.16) | data formatting | bytes 49152 | tf_op jit(solution)/shard_map/reshape | solution.py:385
  (3 shorter events, 0.0 us)
Async XLA Ops:
  0.6 0.9 %copy-start = (f32[3,3,4,512]{3,2,1,0:T(4,128)S(1)}, f32[3,3,4,512]{3,2,1,0:T(4,128)}, u32[]{:S(2)}) copy-start(f32[3,3,4,512]{3,2,1,0:T(4,128)} %param.12) | copy-start | bytes 221188
  39.7 0.7 %copy-start.1 = (f32[3,2,8,128]{3,2,1,0:T(8,128)S(1)}, f32[3,2,8,128]{3,2,1,0:T(8,128)}, u32[]{:S(2)}) copy-start(f32[3,2,8,128]{3,2,1,0:T(8,128)} %get-tuple-element.5) | copy-start | bytes 73732

commit v2 on v1

--- a/solution.py
+++ b/solution.py
@@ -39,7 +39,7 @@
     ang = angles(np.arange(2 * y_all), np.arange(y_all), 2 * y_all)
     y_fwd = np.concatenate([np.cos(ang), -np.sin(ang)])
     z_fwd = np.zeros((ny, 3, 2, NZ, 128))
-    z_inv = np.zeros((ny, 128, 3, 2, NZ))
+    z_inv = np.zeros((ny, 128, 4, NZ))
     for g in range(ny):
         kz = g * block + np.arange(kept)
         ang = angles(np.arange(NZ), kz, 2 * NZ)
@@ -58,16 +58,15 @@
             z_fwd[g, c, 1, :, re] = np.sin(ang)
             z_fwd[g, c, 1, :, im] = np.cos(ang)
             z_fwd[g, c, 0, :, im] = -np.sin(ang)
-            for copy in range(2):
-                z_inv[g, re, c, copy] = (np.cos(ang) * weight).T
-                z_inv[g, im, c, copy] = (-np.sin(ang) * weight).T
+            z_inv[g, re, c] = (np.cos(ang) * weight).T
+            z_inv[g, im, c] = (-np.sin(ang) * weight).T
     z_fwd = z_fwd.reshape(ny, 3 * 2 * NZ, 128)
-    z_inv = z_inv.reshape(ny * 128, 3 * 128)
+    z_inv = z_inv.reshape(ny * 128, 4 * NZ)
     ang = angles(np.arange(2 * x_all), np.arange(x_all), 2 * x_all)
     eye = np.eye(8)
     x_fwd = np.stack([np.cos(ang), np.sin(ang)])
     x_inv = np.einsum("skx,ab->sxabk", x_fwd, eye).reshape(2 * x_all * 8, 8 * 2 * x_all)
-    x_fwd = np.einsum("skx,ab->sakxb", x_fwd, eye).reshape(2 * 8 * 2 * x_all, x_all * 8)
+    x_fwd = np.repeat(x_fwd.reshape(2 * 2 * x_all, x_all), 8, axis=1)
     ang = angles(np.arange(y_all), np.arange(2 * y_all), 2 * y_all)
     y_inv = np.concatenate([np.cos(ang), np.sin(ang)])
     place = np.zeros((3, 2, 3, block, 128))
@@ -118,11 +117,11 @@
 
 def kernel(
     nx, ny,
-    fields, diag_h, off_h, y_fwd_h, z_fwd_h, x_fwd_h, x_inv_h, y_inv_h, z_inv_h, place_h,
+    magnet, thermal, diag_h, off_h, y_fwd_h, z_fwd_h, x_fwd_h, x_inv_h, y_inv_h, z_inv_h, place_h,
     final_ref, demag_ref,
-    diag, off, y_fwd, z_small, z_fwd, x_fwd, x_inv, y_inv, z_inv, place,
+    fields, demag, diag, off, y_fwd, z_small, z_fwd, x_small, x_fwd, x_inv, y_inv, z_inv, place,
     wide, wide_demag, rows_in, spec_out, spec_in, back_out, back_in, row_out, row_in, tensor,
-    local_sem, halo_send, halo_recv, dem_send, dem_recv, ag_send, ag_recv,
+    local_sem, side_send, side_recv, dem_send, dem_recv, ag_send, ag_recv,
     fwd_send, fwd_recv, inv_send, inv_recv, last_send, last_recv,
 ):
     x_all, y_all = nx * LX, ny * LY
@@ -134,7 +133,7 @@
         pltpu.make_async_copy(src, dst, local_sem.at[i])
         for i, (src, dst) in enumerate([
             (y_fwd_h, y_fwd), (z_fwd_h.at[me_y], z_small), (diag_h, diag), (off_h, off),
-            (place_h, place), (x_fwd_h, x_fwd), (x_inv_h, x_inv), (y_inv_h, y_inv), (z_inv_h, z_inv),
+            (place_h, place), (x_fwd_h, x_small), (x_inv_h, x_inv), (y_inv_h, y_inv), (z_inv_h, z_inv),
         ])
     ]
     for load in loads:
@@ -143,6 +142,34 @@
     def present(dx, dy):
         x, y = me_x + dx, me_y + dy
         return (x >= 0) & (x < nx) & (y >= 0) & (y < ny)
+
+    lane = lax.broadcasted_iota(jnp.int32, (1, 128), 1)
+    low_half = lane < 64
+    component = lax.rem(lane, 64)
+    turn = jnp.where(low_half, 1.0, -1.0).astype(jnp.float32)
+
+    def spread(to, value):
+        for pair in range(LY // 2):
+            same = value[:, :, 128 * pair : 128 * (pair + 1)]
+            other = pltpu.roll(same, 64, 2)
+            for t in range(LX // 2):
+                for y in range(2):
+                    a, b = (same, other) if y == 0 else (other, same)
+                    fields[to, :, t, pl.ds(2 * pair + y, 1)] = jnp.where(
+                        low_half[None], a[:, 2 * t : 2 * t + 1], b[:, 2 * t + 1 : 2 * t + 2])
+
+    def collapse(ref, c, same):
+        other = pltpu.roll(same, 64, 2)
+        for t in range(LX // 2):
+            for x in range(2):
+                a, b = (same, other) if x == 0 else (other, same)
+                for pair in range(LY // 2):
+                    ref[c, pl.ds(2 * t + x, 1), 128 * pair : 128 * (pair + 1)] = jnp.where(
+                        low_half, a[t, 2 * pair : 2 * pair + 1], b[t, 2 * pair + 1 : 2 * pair + 2])
+
+    spread(0, magnet[...])
+    wide[:, :, 0:3, 1] = jnp.zeros((1 + STEPS, 3, 3, LY, 128), jnp.float32)
+    wide[:, :, 5:8, 1] = jnp.zeros((1 + STEPS, 3, 3, LY, 128), jnp.float32)
 
     barrier = pltpu.get_barrier_semaphore()
     diagonal = [(dx, dy) for dx, dy in OFFSETS if dx and dy]
@@ -172,39 +199,52 @@
     for copy in gather:
         copy.start()
 
-    def halo(i, kind):
+    def side(i):
+        if i < 4:
+            d = (-2, -1, 1, 2)[i]
+            at, first, count = PLACE[-d]
+            many = 2 if abs(d) == 2 else 1 + STEPS
+            src = fields.at[pl.ds(0, many), :, pl.ds(first, count)]
+            dst = wide.at[pl.ds(0, many), :, pl.ds(at, count), 1]
+            return d, 0, src, dst
+        d = (-1, 1)[i - 4]
+        return 0, d, wide.at[:, :, :, 1], wide.at[:, :, :, 1 - d]
+
+    def side_copy(i):
+        dx, dy, src, dst = side(i)
+        return pltpu.make_async_remote_copy(
+            src, dst, side_send.at[i], side_recv.at[i],
+            device_id=(me_x + dx, me_y + dy), device_id_type=MESH)
+
+    def side_start(which):
+        for i in which:
+            @pl.when(present(*side(i)[:2]))
+            def _():
+                side_copy(i).start()
+
+    def side_wait(which):
+        for i in which:
+            dx, dy = side(i)[:2]
+
+            @pl.when(present(dx, dy))
+            def _():
+                side_copy(i).wait_send()
+
+            @pl.when(present(-dx, -dy))
+            def _():
+                side_copy(i).wait_recv()
+
+    def halo(i):
         dx, dy = OFFSETS[i]
         at, first, count = PLACE[-dx]
-        if kind == 0:
-            many = 2 if abs(dx) == 2 else 4
-            src = fields.at[pl.ds(0, many), :, pl.ds(first, count)]
-            dst = wide.at[pl.ds(0, many), :, pl.ds(at, count), 1 - dy]
-            send, recv = halo_send, halo_recv
-        else:
-            src = demag_ref.at[:, pl.ds(first, count)]
-            dst = wide_demag.at[:, pl.ds(at, count), 1 - dy]
-            send, recv = dem_send, dem_recv
         return pltpu.make_async_remote_copy(
-            src, dst, send.at[i], recv.at[i],
+            demag.at[:, pl.ds(first, count)], wide_demag.at[:, pl.ds(at, count), 1 - dy],
+            dem_send.at[i], dem_recv.at[i],
             device_id=(me_x + dx, me_y + dy), device_id_type=MESH)
 
-    def halo_start(kind):
-        for i, (dx, dy) in enumerate(OFFSETS):
-            @pl.when(present(dx, dy))
-            def _():
-                halo(i, kind).start()
-
-    def halo_wait(kind):
-        for i, (dx, dy) in enumerate(OFFSETS):
-            @pl.when(present(dx, dy))
-            def _():
-                halo(i, kind).wait_send()
-
-            @pl.when(present(-dx, -dy))
-            def _():
-                halo(i, kind).wait_recv()
-
-    halo_start(0)
+    for s in range(STEPS):
+        spread(1 + s, thermal[s])
+    side_start(range(4))
     wide[0:4, :, 3:5, 1] = fields[...]
     rows_in[me_y] = fields[0]
 
@@ -223,6 +263,13 @@
     for x in range(2):
         for part in range(6):
             z_fwd[:, pl.ds(128 * part + NZ * x, NZ), 128 * x : 128 * (x + 1)] = z_small[:, pl.ds(NZ * part, NZ)]
+    loads[5].wait()
+    for a in range(8):
+        own = lax.rem(lax.broadcasted_iota(jnp.int32, (1, 1, 8 * x_all), 2), 8) == a
+        own = jnp.where(own, 1.0, 0.0).astype(jnp.bfloat16)
+        for part in range(2):
+            x_fwd[:, pl.ds((part * 8 + a) * 2 * x_all, 2 * x_all)] = (
+                x_small[:, pl.ds(part * 2 * x_all, 2 * x_all)] * own)
     loads[0].wait()
     for copy in gather:
         copy.wait()
@@ -244,14 +291,11 @@
     for copy in forward:
         copy.start()
     spec_in[me_x] = spec_out[me_x]
-    loads[5].wait()
     loads[6].wait()
-    lane = lax.broadcasted_iota(jnp.int32, (1, 128), 1)
-    low_half = lane < 64
-    component = lax.rem(lane, 64)
-    turn = jnp.where(low_half, 1.0, -1.0).astype(jnp.float32)
     for copy in forward:
         copy.wait()
+    side_wait(range(4))
+    side_start((4, 5))
 
     size = 8 * 2 * x_all
     both = dot_left(x_fwd, spec_in[...].reshape(x_all * 8, 128))
@@ -290,15 +334,28 @@
         copy.wait()
     data = jnp.concatenate([row_in[g].reshape(LX * LY, 128) for g in range(ny)], axis=1)
     rows = dot_right(data, z_inv)
+    turned = jnp.concatenate(
+        [pltpu.roll(rows[:, :128], 64, 1), pltpu.roll(rows[:, 128:], 64, 1)], axis=1)
+    for c, (a, b, first) in enumerate(((rows, turned, 0), (turned, rows, 0), (rows, turned, 128))):
+        a, b = a[:, first : first + 128], b[:, first : first + 128]
+        for t in range(2):
+            demag[c, t] = jnp.where(low_half, a[16 * t : 16 * t + 8], b[16 * t + 8 : 16 * t + 16])
+    for i, (dx, dy) in enumerate(OFFSETS):
+        @pl.when(present(dx, dy))
+        def _():
+            halo(i).start()
+    wide_demag[:, 3:5, 1] = demag[...]
     for c in range(3):
-        lanes = slice(c * 128, (c + 1) * 128)
-        for t in range(2):
-            demag_ref[c, t] = jnp.where(
-                low_half, rows[16 * t : 16 * t + 8, lanes], rows[16 * t + 8 : 16 * t + 16, lanes])
-    halo_start(1)
-    wide_demag[:, 3:5, 1] = demag_ref[...]
-    halo_wait(0)
-    halo_wait(1)
+        collapse(demag_ref, c, demag[c])
+    side_wait((4, 5))
+    for i, (dx, dy) in enumerate(OFFSETS):
+        @pl.when(present(dx, dy))
+        def _():
+            halo(i).wait_send()
+
+        @pl.when(present(-dx, -dy))
+        def _():
+            halo(i).wait_recv()
 
     shape = (8, 3 * LY, 128)
     lanes = lax.broadcasted_iota(jnp.int32, shape, 2)
@@ -337,27 +394,28 @@
         norm = jnp.sqrt(u[0] * u[0] + u[1] * u[1] + u[2] * u[2])
         m = [u[c] / norm for c in range(3)]
     for c in range(3):
-        final_ref[c] = m[c][3:5, LY : 2 * LY]
+        collapse(final_ref, c, m[c][3:5, LY : 2 * LY])
 
 
 def body(nx, ny, magnet, thermal, kernel_diag, kernel_off):
     block = 2 * NZ // ny
     x_all, y_all = nx * LX, ny * LY
     consts = tables(nx, ny)
-    fields = jnp.concatenate([magnet[None], thermal])
-    fields = fields.reshape(1 + STEPS, 3, LX // 2, 2, LY, NZ)
-    fields = jnp.swapaxes(fields, 3, 4).reshape(1 + STEPS, 3, LX // 2, LY, 2 * NZ)
     vmem = pl.BlockSpec(memory_space=pltpu.VMEM)
     anyspace = pl.BlockSpec(memory_space=pl.ANY)
-    out = jax.ShapeDtypeStruct((3, LX // 2, LY, 2 * NZ), jnp.float32)
+    out = jax.ShapeDtypeStruct(magnet.shape, jnp.float32)
     f32, bf16 = jnp.float32, jnp.bfloat16
     scratch = [
+        pltpu.VMEM((1 + STEPS, 3, LX // 2, LY, 128), f32),
+        pltpu.VMEM((3, LX // 2, LY, 128), f32),
         pltpu.VMEM(kernel_diag.shape, f32),
         pltpu.VMEM(kernel_off.shape, f32),
         pltpu.VMEM(consts[0].shape, bf16),
         pltpu.VMEM(consts[1].shape[1:], bf16),
         pltpu.VMEM((2, 3 * 2 * 2 * NZ, 256), bf16),
-        *[pltpu.VMEM(c.shape, bf16) for c in consts[2:]],
+        pltpu.VMEM(consts[2].shape, bf16),
+        pltpu.VMEM((2, 2 * 8 * 2 * x_all, 8 * x_all), bf16),
+        *[pltpu.VMEM(c.shape, bf16) for c in consts[3:]],
         pltpu.VMEM((1 + STEPS, 3, 8, 3, LY, 128), f32),
         pltpu.VMEM((3, 8, 3, LY, 128), f32),
         pltpu.VMEM((ny, 3, 2, LY, 128), f32),
@@ -365,26 +423,21 @@
         *[pltpu.VMEM((ny, LX, LY, 128), f32)] * 2,
         pltpu.VMEM((8 * 2 * x_all, 384), f32),
         pltpu.SemaphoreType.DMA((9,)),
-        *[pltpu.SemaphoreType.DMA((len(OFFSETS),))] * 4,
+        *[pltpu.SemaphoreType.DMA((6,))] * 2,
+        *[pltpu.SemaphoreType.DMA((len(OFFSETS),))] * 2,
         *[pltpu.SemaphoreType.DMA((ny,))] * 2,
         *[pltpu.SemaphoreType.DMA((nx,))] * 4,
         *[pltpu.SemaphoreType.DMA((ny,))] * 2,
     ]
-    final, demag = pl.pallas_call(
+    return pl.pallas_call(
         functools.partial(kernel, nx, ny),
         out_shape=(out, out),
-        in_specs=[vmem] + [anyspace] * 9,
+        in_specs=[vmem, vmem] + [anyspace] * 9,
         out_specs=(vmem, vmem),
         scratch_shapes=scratch,
         compiler_params=pltpu.CompilerParams(
             collective_id=0, has_side_effects=True, vmem_limit_bytes=56 * 1024 * 1024),
-    )(fields, kernel_diag, kernel_off, *[jnp.asarray(c) for c in consts])
-
-    def natural(value):
-        value = value.reshape(3, LX // 2, LY, 2, NZ)
-        return jnp.swapaxes(value, 2, 3).reshape(3, LX, LY * NZ)
-
-    return natural(final), natural(demag)
+    )(magnet, thermal, kernel_diag, kernel_off, *[jnp.asarray(c) for c in consts])
 
 
 def solution(mesh):

time: 41.6 us -> 34.9 us (0.84)
  Pallas kernels: 36.2 us -> 32 us
  local copies, waits for them, and re-layouts: 4.21 us -> 1.96 us
    pallas_call x1, Pallas kernels: 36.2 us -> 32 us  [body(): pl.pallas_call(functools.partial(kernel, nx, ny), out_shape=(out, out), i...]
    reshape x5 -> x0, local copies, waits for them, and re-layouts: 3.09 us -> none  [the longest x2 1.38 us: natural(): return jnp.swapaxes(value, 2, 3).reshape(3, LX, LY * NZ)]
    unnamed x4, local copies, waits for them, and re-layouts: 0.04 us -> 1.96 us
    concatenate x4 -> x0, local copies, waits for them, and re-layouts: 1.07 us -> none  [body(): fields = jnp.concatenate([magnet[None], thermal])]
where the time goes in v2:
time: 34.9 us; the launch traced here: 34.7 us
  Pallas kernels  32 us (92%)
  local copies, waits for them, and re-layouts  1.96 us (6%)
  between operations  0.65 us (2%)
    pallas_call x1, Pallas kernels, body(): pl.pallas_call(functools.partial(kernel, nx, ny), out_shape=(out, out), i...  32 us
    unnamed x4, local copies, waits for them, and re-layouts  1.96 us

profile of v2, /device:TPU:1, one launch (start us, length us, event | category | flops | bytes accessed | tf_op | source)
XLA Modules:
  0.0 34.7 jit_solution(18088118880678954826)
XLA Ops:
  0.6 32.0 %shard_map.122 = (f32[3,4,512]{2,1,0:T(4,128)}, f32[3,4,512]{2,1,0:T(4,128)}) custom-call(f32[3,4,512]{2,1,0:T(4,128)} %magnet.1, f32[3,3,4,512]{3,2,1,0:T(4,128)} %thermal.1, f32[3,32,8,64]{3,2,1,0:T(8,128)} %diag_h.1, f32[3,32,8,64]{3,2,1,0:T(8,128)} %off_h.1, bf16[2,128,32]{2,1,0:T(8,128)(2,1)} %constant.14.clone.y_fwd_h, ...), custom_call_target="tpu_custom_call" | custom-call | tf_op jit(solution)/shard_map/pallas_call | solution.py:432
  32.7 0.0 copy-start
  32.7 1.4 %copy.15 = f32[3,4,512]{2,1,0:T(4,128)} copy(f32[3,4,512]{2,1,0:T(4,128)} %get-tuple-element.4) | data formatting | bytes 49152
  34.0 0.0 copy-done
  34.0 0.6 %copy.16 = f32[3,4,512]{2,1,0:T(4,128)} copy(f32[3,4,512]{2,1,0:T(4,128)S(1)} %copy-done) | data formatting | bytes 49152
Async XLA Ops:
  32.7 1.4 %copy-start = (f32[3,4,512]{2,1,0:T(4,128)S(1)}, f32[3,4,512]{2,1,0:T(4,128)}, u32[]{:S(2)}) copy-start(f32[3,4,512]{2,1,0:T(4,128)} %get-tuple-element.5) | copy-start | bytes 73732

commit v3 on v2

--- a/solution.py
+++ b/solution.py
@@ -26,6 +26,11 @@
     high = table.astype(ml_dtypes.bfloat16)
     low = (table - high.astype(np.float32)).astype(ml_dtypes.bfloat16)
     return np.stack([high, low])
+
+
+def beside(table):
+    high, low = halves(table)
+    return np.concatenate([high, low, high], axis=1)
 
 
 def angles(first, second, period):
@@ -81,11 +86,11 @@
     place = place.reshape(3, 6 * block, 128)
     place = np.concatenate([place[0], place[1], place[2]], axis=1).astype(ml_dtypes.bfloat16)
     return (
-        halves(y_fwd),
+        beside(y_fwd),
         np.moveaxis(halves(z_fwd), 0, 1),
         halves(x_fwd),
         halves(x_inv),
-        halves(y_inv),
+        beside(y_inv),
         halves(z_inv),
         place,
     )
@@ -103,12 +108,21 @@
 
 def dot_left(table, data):
     high, low = split(data)
-    return dot(table[0], high) + (dot(table[0], low) + dot(table[1], high))
+    both = dot(table[0], jnp.concatenate([high, low], axis=1))
+    lanes = data.shape[1]
+    return both[:, :lanes] + (both[:, lanes:] + dot(table[1], high))
+
+
+def dot_thin(table, data):
+    high, low = split(data)
+    return dot(table[...], jnp.concatenate([high, high, low], axis=0))
 
 
 def dot_right(data, table):
     high, low = split(data)
-    return dot(high, table[0]) + (dot(low, table[0]) + dot(high, table[1]))
+    both = dot(jnp.concatenate([high, low], axis=0), table[0])
+    rows = data.shape[0]
+    return both[:rows] + (both[rows:] + dot(high, table[1]))
 
 
 def cross(a, b):
@@ -195,6 +209,8 @@
             src, dst, send.at[i], recv.at[i],
             device_id=(lax.rem(me_x + i, nx), me_y), device_id_type=MESH)
 
+    far_first = sorted(range(1, nx), key=lambda i: abs(2 * i - nx))
+
     gather = [along_y(i, fields.at[0], rows_in.at[me_y], ag_send, ag_recv) for i in range(1, ny)]
     for copy in gather:
         copy.start()
@@ -248,6 +264,37 @@
     wide[0:4, :, 3:5, 1] = fields[...]
     rows_in[me_y] = fields[0]
 
+    loads[1].wait()
+    z_fwd[...] = jnp.zeros_like(z_fwd)
+    for x in range(2):
+        for part in range(6):
+            z_fwd[:, pl.ds(128 * part + NZ * x, NZ), 128 * x : 128 * (x + 1)] = z_small[:, pl.ds(NZ * part, NZ)]
+    loads[0].wait()
+    for copy in gather:
+        copy.wait()
+    data = jnp.concatenate(
+        [rows_in[:, c, t].reshape(y_all, 128) for c in range(3) for t in range(2)], axis=1)
+    spectrum = dot_thin(y_fwd, data)
+    joined = []
+    for t in range(2):
+        parts = []
+        for c in range(3):
+            lanes = slice((2 * c + t) * 128, (2 * c + t + 1) * 128)
+            parts += [spectrum[: 2 * y_all, lanes], spectrum[2 * y_all :, lanes]]
+        joined.append(jnp.concatenate(parts, axis=1))
+    planes = dot_right(jnp.concatenate(joined, axis=0), z_fwd)
+    for t in range(2):
+        for x in range(2):
+            piece = planes[t * 2 * y_all : (t + 1) * 2 * y_all, x * 128 : (x + 1) * 128]
+            spec_out[:, 2 * t + x] = piece.reshape(nx, 8, 128)
+    forward = [
+        along_x(i, spec_out.at[lax.rem(me_x + i, nx)], spec_in.at[me_x], fwd_send, fwd_recv)
+        for i in far_first
+    ]
+    for copy in forward:
+        copy.start()
+    spec_in[me_x] = spec_out[me_x]
+
     for i in (2, 3, 4):
         loads[i].wait()
     for y in range(8):
@@ -257,12 +304,6 @@
             both = jnp.concatenate([high, low], axis=0)
             tensor[pl.ds(y * 2 * x_all, 2 * x_all), first:last] = lax.dot_general(
                 both, place[:, first:last], (((0,), (0,)), ((), ())), preferred_element_type=jnp.float32)
-
-    loads[1].wait()
-    z_fwd[...] = jnp.zeros_like(z_fwd)
-    for x in range(2):
-        for part in range(6):
-            z_fwd[:, pl.ds(128 * part + NZ * x, NZ), 128 * x : 128 * (x + 1)] = z_small[:, pl.ds(NZ * part, NZ)]
     loads[5].wait()
     for a in range(8):
         own = lax.rem(lax.broadcasted_iota(jnp.int32, (1, 1, 8 * x_all), 2), 8) == a
@@ -270,27 +311,6 @@
         for part in range(2):
             x_fwd[:, pl.ds((part * 8 + a) * 2 * x_all, 2 * x_all)] = (
                 x_small[:, pl.ds(part * 2 * x_all, 2 * x_all)] * own)
-    loads[0].wait()
-    for copy in gather:
-        copy.wait()
-    data = jnp.concatenate(
-        [rows_in[:, c, t].reshape(y_all, 128) for c in range(3) for t in range(2)], axis=1)
-    spectrum = dot_left(y_fwd, data)
-    for t in range(2):
-        parts = []
-        for c in range(3):
-            lanes = slice((2 * c + t) * 128, (2 * c + t + 1) * 128)
-            parts += [spectrum[: 2 * y_all, lanes], spectrum[2 * y_all :, lanes]]
-        planes = dot_right(jnp.concatenate(parts, axis=1), z_fwd)
-        for x in range(2):
-            spec_out[:, 2 * t + x] = planes[:, x * 128 : (x + 1) * 128].reshape(nx, 8, 128)
-    forward = [
-        along_x(i, spec_out.at[lax.rem(me_x + i, nx)], spec_in.at[me_x], fwd_send, fwd_recv)
-        for i in range(1, nx)
-    ]
-    for copy in forward:
-        copy.start()
-    spec_in[me_x] = spec_out[me_x]
     loads[6].wait()
     for copy in forward:
         copy.wait()
@@ -308,7 +328,7 @@
     back_out[...] = back.reshape(nx, LX, 8, 128)
     inverse = [
         along_x(i, back_out.at[lax.rem(me_x + i, nx)], back_in.at[me_x], inv_send, inv_recv)
-        for i in range(1, nx)
+        for i in far_first
     ]
     for copy in inverse:
         copy.start()
@@ -318,7 +338,7 @@
     for copy in inverse:
         copy.wait()
     data = jnp.concatenate([back_in[:, x].reshape(nx * 8, 128) for x in range(LX)], axis=1)
-    both = dot_left(y_inv, data)
+    both = dot_thin(y_inv, data)
     for x in range(LX):
         lanes = slice(x * 128, (x + 1) * 128)
         rows = both[:y_all, lanes] - turn * pltpu.roll(both[y_all:, lanes], 64, 1)

time: 34.9 us -> 34.6 us (level)
  Pallas kernels: 32 us -> 31.4 us
    pallas_call x1, Pallas kernels: 32 us -> 31.4 us  [body(): pl.pallas_call(functools.partial(kernel, nx, ny), out_shape=(out, out), i...]
where the time goes in v3:
time: 34.6 us; the launch traced here: 34 us
  Pallas kernels  31.4 us (91%)
  local copies, waits for them, and re-layouts  1.96 us (6%)
  between operations  0.65 us (2%)
    pallas_call x1, Pallas kernels, body(): pl.pallas_call(functools.partial(kernel, nx, ny), out_shape=(out, out), i...  31.4 us
    unnamed x4, local copies, waits for them, and re-layouts  1.96 us

profile of v3, /device:TPU:1, one launch (start us, length us, event | category | flops | bytes accessed | tf_op | source)
XLA Modules:
  0.0 34.0 jit_solution(9470864104803369090)
XLA Ops:
  0.6 31.4 %shard_map.122 = (f32[3,4,512]{2,1,0:T(4,128)}, f32[3,4,512]{2,1,0:T(4,128)}) custom-call(f32[3,4,512]{2,1,0:T(4,128)} %magnet.1, f32[3,3,4,512]{3,2,1,0:T(4,128)} %thermal.1, f32[3,32,8,64]{3,2,1,0:T(8,128)} %diag_h.1, f32[3,32,8,64]{3,2,1,0:T(8,128)} %off_h.1, bf16[128,96]{1,0:T(8,128)(2,1)} %constant.14.clone.y_fwd_h, ...), custom_call_target="tpu_custom_call" | custom-call | tf_op jit(solution)/shard_map/pallas_call | solution.py:452
  32.1 0.0 copy-start
  32.1 1.4 %copy.15 = f32[3,4,512]{2,1,0:T(4,128)} copy(f32[3,4,512]{2,1,0:T(4,128)} %get-tuple-element.4) | data formatting | bytes 49152
  33.4 0.0 copy-done
  33.4 0.6 %copy.16 = f32[3,4,512]{2,1,0:T(4,128)} copy(f32[3,4,512]{2,1,0:T(4,128)S(1)} %copy-done) | data formatting | bytes 49152
Async XLA Ops:
  32.1 1.4 %copy-start = (f32[3,4,512]{2,1,0:T(4,128)S(1)}, f32[3,4,512]{2,1,0:T(4,128)}, u32[]{:S(2)}) copy-start(f32[3,4,512]{2,1,0:T(4,128)} %get-tuple-element.5) | copy-start | bytes 73732

commit v4 on v3

--- a/solution.py
+++ b/solution.py
@@ -150,8 +150,8 @@
             (place_h, place), (x_fwd_h, x_small), (x_inv_h, x_inv), (y_inv_h, y_inv), (z_inv_h, z_inv),
         ])
     ]
-    for load in loads:
-        load.start()
+    for i in (1, 0):
+        loads[i].start()
 
     def present(dx, dy):
         x, y = me_x + dx, me_y + dy
@@ -261,6 +261,8 @@
     for s in range(STEPS):
         spread(1 + s, thermal[s])
     side_start(range(4))
+    for i in (4, 2, 3, 5):
+        loads[i].start()
     wide[0:4, :, 3:5, 1] = fields[...]
     rows_in[me_y] = fields[0]
 
@@ -293,6 +295,8 @@
     ]
     for copy in forward:
         copy.start()
+    for i in (6, 7, 8):
+        loads[i].start()
     spec_in[me_x] = spec_out[me_x]
 
     for i in (2, 3, 4):

time: 34.6 us -> 34.6 us (level)
  no operation moved by 1% of the time
where the time goes in v4:
time: 34.6 us; the launch traced here: 34 us
  Pallas kernels  31.4 us (91%)
  local copies, waits for them, and re-layouts  1.96 us (6%)
  between operations  0.65 us (2%)
    pallas_call x1, Pallas kernels, body(): pl.pallas_call(functools.partial(kernel, nx, ny), out_shape=(out, out), i...  31.4 us
    unnamed x4, local copies, waits for them, and re-layouts  1.96 us

profile of v4, /device:TPU:1, one launch (start us, length us, event | category | flops | bytes accessed | tf_op | source)
XLA Modules:
  0.0 34.0 jit_solution(7077528178184140058)
XLA Ops:
  0.6 31.4 %shard_map.122 = (f32[3,4,512]{2,1,0:T(4,128)}, f32[3,4,512]{2,1,0:T(4,128)}) custom-call(f32[3,4,512]{2,1,0:T(4,128)} %magnet.1, f32[3,3,4,512]{3,2,1,0:T(4,128)} %thermal.1, f32[3,32,8,64]{3,2,1,0:T(8,128)} %diag_h.1, f32[3,32,8,64]{3,2,1,0:T(8,128)} %off_h.1, bf16[128,96]{1,0:T(8,128)(2,1)} %constant.14.clone.y_fwd_h, ...), custom_call_target="tpu_custom_call" | custom-call | tf_op jit(solution)/shard_map/pallas_call | solution.py:456
  32.1 0.0 copy-start
  32.1 1.4 %copy.15 = f32[3,4,512]{2,1,0:T(4,128)} copy(f32[3,4,512]{2,1,0:T(4,128)} %get-tuple-element.4) | data formatting | bytes 49152
  33.4 0.0 copy-done
  33.4 0.6 %copy.16 = f32[3,4,512]{2,1,0:T(4,128)} copy(f32[3,4,512]{2,1,0:T(4,128)S(1)} %copy-done) | data formatting | bytes 49152
Async XLA Ops:
  32.1 1.4 %copy-start = (f32[3,4,512]{2,1,0:T(4,128)S(1)}, f32[3,4,512]{2,1,0:T(4,128)}, u32[]{:S(2)}) copy-start(f32[3,4,512]{2,1,0:T(4,128)} %get-tuple-element.5) | copy-start | bytes 73732

commit v5 on v4

--- a/solution.py
+++ b/solution.py
@@ -181,7 +181,6 @@
                     ref[c, pl.ds(2 * t + x, 1), 128 * pair : 128 * (pair + 1)] = jnp.where(
                         low_half, a[t, 2 * pair : 2 * pair + 1], b[t, 2 * pair + 1 : 2 * pair + 2])
 
-    spread(0, magnet[...])
     wide[:, :, 0:3, 1] = jnp.zeros((1 + STEPS, 3, 3, LY, 128), jnp.float32)
     wide[:, :, 5:8, 1] = jnp.zeros((1 + STEPS, 3, 3, LY, 128), jnp.float32)
 
@@ -197,6 +196,9 @@
             pl.semaphore_signal(barrier, 1, device_id=(me_x + dx, me_y + dy), device_id_type=MESH)
     beside_x = jnp.minimum(me_x, 2) + jnp.minimum(nx - 1 - me_x, 2)
     beside_y = jnp.minimum(me_y, 1) + jnp.minimum(ny - 1 - me_y, 1)
+    spread(0, magnet[...])
+    for s in range(STEPS):
+        spread(1 + s, thermal[s])
     pl.semaphore_wait(barrier, nx + ny - 2 + beside_x * beside_y)
 
     def along_y(i, src, dst, send, recv):
@@ -258,8 +260,6 @@
             dem_send.at[i], dem_recv.at[i],
             device_id=(me_x + dx, me_y + dy), device_id_type=MESH)
 
-    for s in range(STEPS):
-        spread(1 + s, thermal[s])
     side_start(range(4))
     for i in (4, 2, 3, 5):
         loads[i].start()

time: 34.6 us -> 34.5 us (level)
  no operation moved by 1% of the time
where the time goes in v5:
time: 34.5 us; the launch traced here: 34 us
  Pallas kernels  31.4 us (91%)
  local copies, waits for them, and re-layouts  1.96 us (6%)
  between operations  0.65 us (2%)
    pallas_call x1, Pallas kernels, body(): pl.pallas_call(functools.partial(kernel, nx, ny), out_shape=(out, out), i...  31.4 us
    unnamed x4, local copies, waits for them, and re-layouts  1.96 us

profile of v5, /device:TPU:1, one launch (start us, length us, event | category | flops | bytes accessed | tf_op | source)
XLA Modules:
  0.0 34.0 jit_solution(14744494868085269243)
XLA Ops:
  0.6 31.4 %shard_map.122 = (f32[3,4,512]{2,1,0:T(4,128)}, f32[3,4,512]{2,1,0:T(4,128)}) custom-call(f32[3,4,512]{2,1,0:T(4,128)} %magnet.1, f32[3,3,4,512]{3,2,1,0:T(4,128)} %thermal.1, f32[3,32,8,64]{3,2,1,0:T(8,128)} %diag_h.1, f32[3,32,8,64]{3,2,1,0:T(8,128)} %off_h.1, bf16[128,96]{1,0:T(8,128)(2,1)} %constant.14.clone.y_fwd_h, ...), custom_call_target="tpu_custom_call" | custom-call | tf_op jit(solution)/shard_map/pallas_call | solution.py:456
  32.0 0.0 copy-start
  32.0 1.4 %copy.15 = f32[3,4,512]{2,1,0:T(4,128)} copy(f32[3,4,512]{2,1,0:T(4,128)} %get-tuple-element.4) | data formatting | bytes 49152
  33.4 0.0 copy-done
  33.4 0.6 %copy.16 = f32[3,4,512]{2,1,0:T(4,128)} copy(f32[3,4,512]{2,1,0:T(4,128)S(1)} %copy-done) | data formatting | bytes 49152
Async XLA Ops:
  32.0 1.4 %copy-start = (f32[3,4,512]{2,1,0:T(4,128)S(1)}, f32[3,4,512]{2,1,0:T(4,128)}, u32[]{:S(2)}) copy-start(f32[3,4,512]{2,1,0:T(4,128)} %get-tuple-element.5) | copy-start | bytes 73732
